TPU v7x, 512 devices: a whole 4x8x8 slice. The times are simulated.
512 devices in a mesh: span: 64 (over x, z, core), elem: 8 (over y).
Axes of the slice: x: 4, y: 8, z: 8, core: 2. Of those that a mesh axis runs over, the one named last changes fastest.
Arguments:
- current_block: float32 [64, 64, 20480], P('span', None, 'elem'), may hold values from -6 to 6
- search_block: float32 [64, 64, 20480], P('span', None, 'elem'), may hold values from -6 to 6
- previous_block: float32 [64, 64, 20480], P('span', None, 'elem'), may hold values from -6 to 6
- ground_spring: float32 [20480], P('elem'), may hold values from 1 to 18
- wire_tension: float32 [20480], P('elem'), may hold values from 0.3 to 13.5
- dropper_stiff: float32 [20480], P('elem'), may hold values from 0.3 to 3
- dropper_offset: int32 [20480], P('elem'), may hold values from 1 to 8
- span_link: float32 [20480], P('elem'), may hold values from 0.1 to 0.4
- ritz_rotation: float32 [64, 192, 64], P('span'), may hold values from -0.4375 to 0.4375
Outputs:
- next_block: float32 [64, 64, 20480], P('span', None, 'elem')
- next_residual: float32 [64, 64, 20480], P('span', None, 'elem')
- ritz_values: float32 [64, 64], P('span')
Inputs may be any that keep to these rules, and one draw needn't show every extreme that they name: `dropper_offset`: 20480 * i is joined by a dropper to 20480 * i + dropper_offset_i; droppers that would reach past 20480 20480 - 1 are absent.
All inputs are finite; a program needn't handle non-finite values.
Results may differ from a plain program's by a relative error of at most 0.00016.
Values sent between devices are 32-bit elements; how exact they have to be, the bound alone decides.
A program may use at most 128 MiB of HBM per device.

v0:
```python
import math

import jax
import jax.numpy as jnp
from jax import lax
from jax.sharding import PartitionSpec as P

REACH = 8


def shifted(value, axis, steps):
    count = lax.axis_size(axis)
    leading, last = (max(0, -steps), min(count, count - steps))
    return lax.ppermute(value, axis, [(source, source + steps) for source in range(leading, last)])


def with_halo(cells, sides, width):
    for axis, dim in sides:
        count = lax.axis_size(axis)
        ends = count - 1
        head = lax.slice_in_dim(cells, 0, width, axis=dim)
        tail = lax.slice_in_dim(cells, cells.shape[dim] - width, cells.shape[dim], axis=dim)
        cells = jnp.concatenate(
            [
                lax.ppermute(tail, axis, [(i, (i + 1) % count) for i in range(ends)]),
                cells,
                lax.ppermute(head, axis, [((i + 1) % count, i) for i in range(ends)]),
            ],
            axis=dim,
        )
    return cells


def fourier_rows(count):
    row = jnp.arange(count)[:, None]
    col = jnp.arange(count)[None, :]
    half = count // 2
    wave = jnp.where(row <= half, row, row - half)
    phase = (wave * col % count).astype(jnp.float32) * (2.0 * math.pi / count)
    scaled = jnp.where(row <= half, jnp.cos(phase), jnp.sin(phase)) * math.sqrt(2.0 / count)
    edge = (row == 0) | (row == half)
    matrix = jnp.where(edge, jnp.cos(phase) * math.sqrt(1.0 / count), scaled)
    slots = jnp.arange(count)
    slot_wave = jnp.where(slots <= half, slots, slots - half)
    cosines = jnp.cos(slot_wave.astype(jnp.float32) * (2.0 * math.pi / count))
    return (matrix, cosines)


def along_spans(matrix, block):
    shape = block.shape
    flat = block.reshape(shape[0], -1)
    return jnp.dot(matrix, flat, precision=lax.Precision.HIGHEST).reshape(shape)


def on_device(
    current_block,
    search_block,
    previous_block,
    ground_spring,
    wire_tension,
    dropper_stiff,
    dropper_offset,
    span_link,
    ritz_rotation,
):
    reach = REACH
    span_dev = current_block.shape[0]
    dof_dev = current_block.shape[2]
    total = span_dev * lax.axis_size("span")
    matrix, cosines = fourier_rows(total)
    my_cosines = lax.dynamic_slice_in_dim(cosines, lax.axis_index("span") * span_dev, span_dev)
    gathered = (
        lax.all_to_all(current_block, "span", split_axis=1, concat_axis=0, tiled=True),
        lax.all_to_all(search_block, "span", split_axis=1, concat_axis=0, tiled=True),
        lax.all_to_all(previous_block, "span", split_axis=1, concat_axis=0, tiled=True),
    )
    moved = [along_spans(matrix, piece) for piece in gathered]
    slot_x, slot_w, slot_p = (
        lax.all_to_all(moved[0], "span", split_axis=0, concat_axis=1, tiled=True),
        lax.all_to_all(moved[1], "span", split_axis=0, concat_axis=1, tiled=True),
        lax.all_to_all(moved[2], "span", split_axis=0, concat_axis=1, tiled=True),
    )
    stacked = jnp.concatenate([slot_x, slot_w, slot_p], 1)
    position = lax.axis_index("elem") * dof_dev + jnp.arange(dof_dev)
    dof_all = dof_dev * lax.axis_size("elem")
    tension_here = jnp.where(position < dof_all - 1, wire_tension, 0.0)
    dropper_rows = jnp.stack(
        [
            jnp.where(
                (dropper_offset == distance) & (position + distance < dof_all), dropper_stiff, 0.0
            )
            for distance in range(1, reach + 1)
        ]
    )
    left_tension, left_rows = shifted(
        (tension_here[dof_dev - 1 :], dropper_rows[:, dof_dev - reach :]), "elem", 1
    )
    extended = with_halo(stacked, (("elem", 2),), reach)
    center = extended[:, :, reach : reach + dof_dev]
    tensions = jnp.concatenate([left_tension, tension_here])
    flux = tensions * (
        extended[:, :, reach - 1 : reach + dof_dev] - extended[:, :, reach : reach + dof_dev + 1]
    )
    applied = ground_spring * center + flux[:, :, 1:] - flux[:, :, :-1]
    rows_all = jnp.concatenate([left_rows, dropper_rows], 1)
    near = extended[:, :, : reach + dof_dev]
    for distance in range(1, reach + 1):
        flux = rows_all[distance - 1] * (
            near - extended[:, :, distance : distance + reach + dof_dev]
        )
        applied = (
            applied + flux[:, :, reach:] - flux[:, :, reach - distance : reach - distance + dof_dev]
        )
    applied = applied + (2.0 * (1.0 - my_cosines))[:, None, None] * span_link * center
    projected = jnp.einsum("sjm,sjd->smd", ritz_rotation, stacked, precision=lax.Precision.HIGHEST)
    stiff_projected = jnp.einsum(
        "sjm,sjd->smd", ritz_rotation, applied, precision=lax.Precision.HIGHEST
    )
    gram_stiff = jnp.einsum("sjd,skd->sjk", stacked, applied, precision=lax.Precision.HIGHEST)
    gram_plain = jnp.einsum("sjd,skd->sjk", stacked, stacked, precision=lax.Precision.HIGHEST)
    gram_stiff, gram_plain = lax.psum((gram_stiff, gram_plain), "elem")
    energy = jnp.einsum(
        "sjm,sjk,skm->sm", ritz_rotation, gram_stiff, ritz_rotation, precision=lax.Precision.HIGHEST
    )
    weight_sum = jnp.einsum(
        "sjm,sjk,skm->sm", ritz_rotation, gram_plain, ritz_rotation, precision=lax.Precision.HIGHEST
    )
    ritz = energy / (weight_sum + 1e-06)
    residual = stiff_projected - ritz[:, :, None] * projected
    back_matrix = matrix.T
    gathered = (
        lax.all_to_all(projected, "span", split_axis=1, concat_axis=0, tiled=True),
        lax.all_to_all(residual, "span", split_axis=1, concat_axis=0, tiled=True),
    )
    moved = [along_spans(back_matrix, piece) for piece in gathered]
    next_block, next_residual = (
        lax.all_to_all(moved[0], "span", split_axis=0, concat_axis=1, tiled=True),
        lax.all_to_all(moved[1], "span", split_axis=0, concat_axis=1, tiled=True),
    )
    return (next_block, next_residual, ritz)


def solution(mesh):
    return jax.shard_map(
        on_device,
        mesh=mesh,
        in_specs=(
            P("span", None, "elem"),
            P("span", None, "elem"),
            P("span", None, "elem"),
            P("elem"),
            P("elem"),
            P("elem"),
            P("elem"),
            P("elem"),
            P("span", None, None),
        ),
        out_specs=(P("span", None, "elem"), P("span", None, "elem"), P("span", None)),
        check_vma=False,
    )
```

profile of v0, /device:TPU:1, one launch (start us, length us, event | category | flops | bytes accessed | tf_op | source)
XLA Modules:
  0.0 511.1 jit_solution(5302990973566107633)
XLA Ops:
  9.8 15.0 %all-to-all-start = ((f32[1,64,2560]{2,0,1:T(1,128)}), f32[1,64,2560]{2,0,1:T(1,128)S(1)}, u32[]{:S(2)}, u32[]{:S(2)}) async-start(f32[1,64,2560]{2,0,1:T(1,128)} %copy.24), calls=%async_computation | async-start | bytes 1310720 | tf_op jit(solution)/shard_map/all_to_all | solution.py:73
  26.3 18.6 %all-to-all-done = f32[1,64,2560]{2,0,1:T(1,128)S(1)} async-done(((f32[1,64,2560]{2,0,1:T(1,128)}), f32[1,64,2560]{2,0,1:T(1,128)S(1)}, u32[]{:S(2)}, u32[]{:S(2)}) %all-to-all-start) | async-done | bytes 655392 | tf_op jit(solution)/shard_map/all_to_all | solution.py:73
  44.9 6.3 %all-to-all-start.2 = ((f32[1,64,2560]{2,0,1:T(1,128)}), f32[1,64,2560]{2,0,1:T(1,128)S(1)}, u32[]{:S(2)}, u32[]{:S(2)}) async-start(f32[1,64,2560]{2,0,1:T(1,128)} %copy.26), calls=%async_computation.2 | async-start | bytes 1310720 | tf_op jit(solution)/shard_map/all_to_all | solution.py:74
  52.7 18.6 %all-to-all-done.2 = f32[1,64,2560]{2,0,1:T(1,128)S(1)} async-done(((f32[1,64,2560]{2,0,1:T(1,128)}), f32[1,64,2560]{2,0,1:T(1,128)S(1)}, u32[]{:S(2)}, u32[]{:S(2)}) %all-to-all-start.2) | async-done | bytes 655392 | tf_op jit(solution)/shard_map/all_to_all | solution.py:74
  71.3 6.3 %all-to-all-start.4 = ((f32[1,64,2560]{2,0,1:T(1,128)}), f32[1,64,2560]{2,0,1:T(1,128)S(1)}, u32[]{:S(2)}, u32[]{:S(2)}) async-start(f32[1,64,2560]{2,0,1:T(1,128)} %copy.28), calls=%async_computation.4 | async-start | bytes 1310720 | tf_op jit(solution)/shard_map/all_to_all | solution.py:75
  80.0 17.7 %all-to-all-done.4 = f32[1,64,2560]{2,0,1:T(1,128)S(1)} async-done(((f32[1,64,2560]{2,0,1:T(1,128)}), f32[1,64,2560]{2,0,1:T(1,128)S(1)}, u32[]{:S(2)}, u32[]{:S(2)}) %all-to-all-start.4) | async-done | bytes 655392 | tf_op jit(solution)/shard_map/all_to_all | solution.py:75
  97.7 6.3 %all-to-all-start.1 = ((f32[64,1,2560]{2,1,0:T(1,128)}), f32[64,1,2560]{2,1,0:T(1,128)S(1)}, u32[]{:S(2)}, u32[]{:S(2)}) async-start(f32[64,1,2560]{2,1,0:T(1,128)} %copy.25), calls=%async_computation.1 | async-start | bytes 1310720 | tf_op jit(solution)/shard_map/all_to_all | solution.py:79
  106.4 17.7 %all-to-all-done.1 = f32[64,1,2560]{2,1,0:T(1,128)S(1)} async-done(((f32[64,1,2560]{2,1,0:T(1,128)}), f32[64,1,2560]{2,1,0:T(1,128)S(1)}, u32[]{:S(2)}, u32[]{:S(2)}) %all-to-all-start.1) | async-done | bytes 655392 | tf_op jit(solution)/shard_map/all_to_all | solution.py:79
  124.1 6.3 %all-to-all-start.3 = ((f32[64,1,2560]{2,1,0:T(1,128)}), f32[64,1,2560]{2,1,0:T(1,128)S(1)}, u32[]{:S(2)}, u32[]{:S(2)}) async-start(f32[64,1,2560]{2,1,0:T(1,128)} %copy.27), calls=%async_computation.3 | async-start | bytes 1310720 | tf_op jit(solution)/shard_map/all_to_all | solution.py:80
  132.9 17.7 %all-to-all-done.3 = f32[64,1,2560]{2,1,0:T(1,128)S(1)} async-done(((f32[64,1,2560]{2,1,0:T(1,128)}), f32[64,1,2560]{2,1,0:T(1,128)S(1)}, u32[]{:S(2)}, u32[]{:S(2)}) %all-to-all-start.3) | async-done | bytes 655392 | tf_op jit(solution)/shard_map/all_to_all | solution.py:80
  150.5 6.5 %all-to-all-start.5 = ((f32[64,1,2560]{2,1,0:T(1,128)}), f32[64,1,2560]{2,1,0:T(1,128)S(1)}, u32[]{:S(2)}, u32[]{:S(2)}) async-start(f32[64,1,2560]{2,1,0:T(1,128)} %copy.29), calls=%async_computation.5 | async-start | bytes 1310720 | tf_op jit(solution)/shard_map/all_to_all | solution.py:81
  168.4 8.7 %all-to-all-done.5 = f32[64,1,2560]{2,1,0:T(1,128)S(1)} async-done(((f32[64,1,2560]{2,1,0:T(1,128)}), f32[64,1,2560]{2,1,0:T(1,128)S(1)}, u32[]{:S(2)}, u32[]{:S(2)}) %all-to-all-start.5) | async-done | bytes 655392 | tf_op jit(solution)/shard_map/all_to_all | solution.py:81
  189.1 6.7 %all-to-all-start.6 = ((f32[1,64,2560]{2,0,1:T(1,128)}), f32[1,64,2560]{2,0,1:T(1,128)}, u32[]{:S(2)}, u32[]{:S(2)}) async-start(f32[1,64,2560]{2,0,1:T(1,128)} %copy.30), calls=%async_computation.6 | async-start | bytes 1310720 | tf_op jit(solution)/shard_map/all_to_all | solution.py:132
  196.3 13.4 %concatenate.53 = f32[1,192,2576]{2,0,1:T(1,128)S(1)} concatenate(f32[1,192,8]{2,0,1:T(1,128)S(1)} %collective-permute-done.1, f32[1,192,2560]{2,0,1:T(1,128)} %copy-done, f32[1,192,8]{2,0,1:T(1,128)} %collective-permute-done.2), dimensions={2} | concatenate | bytes 3956736 | tf_op jit(solution)/shard_map/concatenate | solution.py:23
  209.7 18.9 %fusion.8 = (f32[1,192,2568]{2,0,1:T(1,128)S(1)}, f32[1,192,2568]{2,0,1:T(1,128)S(1)}) fusion(f32[1,192,2576]{2,0,1:T(1,128)S(1)} %concatenate.53, f32[2568]{0:T(1024)} %get-tuple-element.9, f32[1,64,2560]{2,0,1:T(1,128)} %bitcast.96, f32[1,64,2560]{2,0,1:T(1,128)S(1)} %bitcast.92, f32[1,64,2560]{2,0,1:T(1,128)S(1)} %bitcast.88, ...), kind=kLoop, calls=%fused_computation.21 | loop fusion | flops 2465280 | bytes 7899168 | tf_op jit(solution)/shard_map/mul | solution.py:108
  228.7 30.0 %fusion.7 = (f32[1,192,2568]{2,0,1:T(1,128)S(1)}, f32[1,192,2568]{2,0,1:T(1,128)S(1)}, f32[1,192,2568]{2,0,1:T(1,128)S(1)}, f32[1,192,2568]{2,0,1:T(1,128)S(1)},...) fusion(f32[1,192,2568]{2,0,1:T(1,128)S(1)} %get-tuple-element.2, ...), kind=kLoop, calls=%fused_computation.19 | loop fusion | flops 8381952 | bytes 31627488 | tf_op jit(solution)/shard_map/mul | solution.py:108
  263.1 66.4 %fusion.10 = f32[1,192,2560]{2,0,1:T(1,128)S(1)} fusion(f32[1,192,2568]{2,0,1:T(1,128)S(1)} %get-tuple-element.29, f32[1,192,2568]{2,0,1:T(1,128)S(1)} %get-tuple-element.24, f32[1,192,2568]{2,0,1:T(1,128)S(1)} %get-tuple-element.25, f32[1,192,2568]{2,0,1:T(1,128)S(1)} %get-tuple-element.26, f32[1,192,2568]{2,0,1:T(1,128)S(1)} %get-tuple-element.27, ...), kind=kLoop, calls=%fused_computation.28 | loop fusion | flops 11304960 | bytes 39342080 | tf_op jit(solution)/shard_map/add | solution.py:114
  331.9 77.0 %all-reduce.3.cloned.1.call-done = (f32[192,192]{1,0:T(8,128)}, f32[192,192]{1,0:T(8,128)}) async-done(((f32[192,192]{1,0:T(8,128)}, f32[192,192]{1,0:T(8,128)}), (f32[192,192]{1,0:T(8,128)}, f32[192,192]{1,0:T(8,128)})) %all-reduce.3.cloned.1.call-update) | async-done | bytes 294928 | tf_op jit(solution)/shard_map/psum | solution.py:121
  414.5 15.8 %all-to-all-start.8 = ((f32[1,64,2560]{2,0,1:T(1,128)}), f32[1,64,2560]{2,0,1:T(1,128)S(1)}, u32[]{:S(2)}, u32[]{:S(2)}) async-start(f32[1,64,2560]{2,0,1:T(1,128)} %copy.32), calls=%async_computation.8 | async-start | bytes 1310720 | tf_op jit(solution)/shard_map/all_to_all | solution.py:133
  433.8 16.6 %all-to-all-done.8 = f32[1,64,2560]{2,0,1:T(1,128)S(1)} async-done(((f32[1,64,2560]{2,0,1:T(1,128)}), f32[1,64,2560]{2,0,1:T(1,128)S(1)}, u32[]{:S(2)}, u32[]{:S(2)}) %all-to-all-start.8) | async-done | bytes 655392 | tf_op jit(solution)/shard_map/all_to_all | solution.py:133
  450.4 6.3 %all-to-all-start.7 = ((f32[64,1,2560]{2,1,0:T(1,128)}), f32[64,1,2560]{2,1,0:T(1,128)S(1)}, u32[]{:S(2)}, u32[]{:S(2)}) async-start(f32[64,1,2560]{2,1,0:T(1,128)} %copy.31), calls=%async_computation.7 | async-start | bytes 1310720 | tf_op jit(solution)/shard_map/all_to_all | solution.py:137
  459.1 17.7 %all-to-all-done.7 = f32[64,1,2560]{2,1,0:T(1,128)S(1)} async-done(((f32[64,1,2560]{2,1,0:T(1,128)}), f32[64,1,2560]{2,1,0:T(1,128)S(1)}, u32[]{:S(2)}, u32[]{:S(2)}) %all-to-all-start.7) | async-done | bytes 655392 | tf_op jit(solution)/shard_map/all_to_all | solution.py:137
  476.8 6.3 %all-to-all-start.9 = ((f32[64,1,2560]{2,1,0:T(1,128)}), f32[64,1,2560]{2,1,0:T(1,128)S(1)}, u32[]{:S(2)}, u32[]{:S(2)}) async-start(f32[64,1,2560]{2,1,0:T(1,128)} %copy.33), calls=%async_computation.9 | async-start | bytes 1310720 | tf_op jit(solution)/shard_map/all_to_all | solution.py:138
  483.9 19.2 %all-to-all-done.9 = f32[64,1,2560]{2,1,0:T(1,128)S(1)} async-done(((f32[64,1,2560]{2,1,0:T(1,128)}), f32[64,1,2560]{2,1,0:T(1,128)S(1)}, u32[]{:S(2)}, u32[]{:S(2)}) %all-to-all-start.9) | async-done | bytes 655392 | tf_op jit(solution)/shard_map/all_to_all | solution.py:138
  (112 shorter events, 55.9 us)
Async XLA Ops:
  9.8 41.4 %copy-start.8 = (f32[1,64,2560]{2,1,0:T(8,128)S(1)}, f32[1,64,2560]{2,1,0:T(8,128)}, u32[]{:S(2)}) copy-start(f32[1,64,2560]{2,1,0:T(8,128)} %param.11) | copy-start | bytes 1966084
  9.8 35.1 %all-to-all-start = ((f32[1,64,2560]{2,0,1:T(1,128)}), f32[1,64,2560]{2,0,1:T(1,128)S(1)}, u32[]{:S(2)}, u32[]{:S(2)}) async-start(f32[1,64,2560]{2,0,1:T(1,128)} %copy.24), calls=%async_computation | async-start | bytes 1310720 | tf_op jit(solution)/shard_map/all_to_all | solution.py:73
  44.9 26.4 %all-to-all-start.2 = ((f32[1,64,2560]{2,0,1:T(1,128)}), f32[1,64,2560]{2,0,1:T(1,128)S(1)}, u32[]{:S(2)}, u32[]{:S(2)}) async-start(f32[1,64,2560]{2,0,1:T(1,128)} %copy.26), calls=%async_computation.2 | async-start | bytes 1310720 | tf_op jit(solution)/shard_map/all_to_all | solution.py:74
  71.3 26.4 %all-to-all-start.4 = ((f32[1,64,2560]{2,0,1:T(1,128)}), f32[1,64,2560]{2,0,1:T(1,128)S(1)}, u32[]{:S(2)}, u32[]{:S(2)}) async-start(f32[1,64,2560]{2,0,1:T(1,128)} %copy.28), calls=%async_computation.4 | async-start | bytes 1310720 | tf_op jit(solution)/shard_map/all_to_all | solution.py:75
  77.6 52.8 %copy-start.17 = (pred[64]{0:T(512)(128)(4,1)}, pred[64]{0:T(512)(128)(4,1)S(1)}, u32[]{:S(2)}) copy-start(pred[64]{0:T(512)(128)(4,1)S(1)} %get-tuple-element.41) | copy-start | bytes 196
  77.6 52.8 %copy-start.19 = (pred[64]{0:T(512)(128)(4,1)}, pred[64]{0:T(512)(128)(4,1)S(1)}, u32[]{:S(2)}) copy-start(pred[64]{0:T(512)(128)(4,1)S(1)} %get-tuple-element.42) | copy-start | bytes 196
  97.7 26.4 %all-to-all-start.1 = ((f32[64,1,2560]{2,1,0:T(1,128)}), f32[64,1,2560]{2,1,0:T(1,128)S(1)}, u32[]{:S(2)}, u32[]{:S(2)}) async-start(f32[64,1,2560]{2,1,0:T(1,128)} %copy.25), calls=%async_computation.1 | async-start | bytes 1310720 | tf_op jit(solution)/shard_map/all_to_all | solution.py:79
  124.1 26.4 %all-to-all-start.3 = ((f32[64,1,2560]{2,1,0:T(1,128)}), f32[64,1,2560]{2,1,0:T(1,128)S(1)}, u32[]{:S(2)}, u32[]{:S(2)}) async-start(f32[64,1,2560]{2,1,0:T(1,128)} %copy.27), calls=%async_computation.3 | async-start | bytes 1310720 | tf_op jit(solution)/shard_map/all_to_all | solution.py:80
  130.4 26.6 %copy-start.24 = (f32[2560]{0:T(1024)S(1)}, f32[2560]{0:T(1024)}, u32[]{:S(2)}) copy-start(f32[2560]{0:T(1024)} %param.14) | copy-start | bytes 30724
  130.4 30.2 %copy-start.22 = (f32[2560]{0:T(1024)S(1)}, f32[2560]{0:T(1024)}, u32[]{:S(2)}) copy-start(f32[2560]{0:T(1024)} %param.13) | copy-start | bytes 30724
  130.5 35.8 %copy-start.23 = (f32[2560]{0:T(1024)S(1)}, f32[2560]{0:T(1024)}, u32[]{:S(2)}) copy-start(f32[2560]{0:T(1024)} %param.16) | copy-start | bytes 30724
  150.5 26.6 %all-to-all-start.5 = ((f32[64,1,2560]{2,1,0:T(1,128)}), f32[64,1,2560]{2,1,0:T(1,128)S(1)}, u32[]{:S(2)}, u32[]{:S(2)}) async-start(f32[64,1,2560]{2,1,0:T(1,128)} %copy.29), calls=%async_computation.5 | async-start | bytes 1310720 | tf_op jit(solution)/shard_map/all_to_all | solution.py:81
  157.4 10.2 %collective-permute-start.3 = (f32[8,8]{1,0:T(8,128)S(1)}, f32[8,8]{1,0:T(8,128)S(1)}, u32[]{:S(2)}, u32[]{:S(2)}) collective-permute-start(f32[8,8]{1,0:T(8,128)S(1)} %slice.169), channel_id=1, source_target_pairs={{0,1},{1,2},{2,3},{3,4},{4,5},{5,6},{6,7},{8,9},{9,10},{10,11},{11... | collective-permute-start | bytes 776 | tf_op jit(solution)/shard_map/ppermute | solution.py:14
  161.2 5.0 collective-permute-start
  179.2 17.1 %collective-permute-start.1 = (f32[1,192,8]{2,0,1:T(1,128)S(1)}, f32[1,192,8]{2,0,1:T(1,128)S(1)}, u32[]{:S(2)}, u32[]{:S(2)}) collective-permute-start(f32[1,192,8]{2,0,1:T(1,128)S(1)} %get-tuple-element.32), channel_id=1, source_target_pairs={{0,1},{1,2},{2,3},{3,4},{4,5},{5,6},{6,7},{8,9},{9,10},{10,11},{11... | collective-permute-start | bytes 18440 | tf_op jit(solution)/shard_map/ppermute | solution.py:25
  182.4 13.9 %collective-permute-start.2 = (f32[1,192,8]{2,0,1:T(1,128)S(1)}, f32[1,192,8]{2,0,1:T(1,128)}, u32[]{:S(2)}, u32[]{:S(2)}) collective-permute-start(f32[1,192,8]{2,0,1:T(1,128)S(1)} %get-tuple-element.31), channel_id=1, source_target_pairs={{1,0},{2,1},{3,2},{4,3},{5,4},{6,5},{7,6},{9,8},{10,9},{11,10},{12... | collective-permute-start | bytes 18440 | tf_op jit(solution)/shard_map/ppermute | solution.py:27
  189.1 225.4 %all-to-all-start.6 = ((f32[1,64,2560]{2,0,1:T(1,128)}), f32[1,64,2560]{2,0,1:T(1,128)}, u32[]{:S(2)}, u32[]{:S(2)}) async-start(f32[1,64,2560]{2,0,1:T(1,128)} %copy.30), calls=%async_computation.6 | async-start | bytes 1310720 | tf_op jit(solution)/shard_map/all_to_all | solution.py:132
  195.8 213.1 %all-reduce.3.cloned.1.call-start = ((), (), s32[]{:S(2)}) async-start(), calls=%async_computation.10 | async-start | bytes 786432 | tf_op jit(solution)/shard_map/psum | solution.py:121
  228.7 30.0 %copy-start.16 = (f32[2561]{0:T(1024)S(1)}, f32[2561]{0:T(1024)}, u32[]{:S(2)}) copy-start(f32[2561]{0:T(1024)} %pad_maximum_fusion.2) | copy-start | bytes 30736
  263.0 66.4 %copy-start.1 = (f32[1,192,2560]{2,0,1:T(1,128)S(1)}, f32[1,192,2560]{2,0,1:T(1,128)}, u32[]{:S(2)}) copy-start(f32[1,192,2560]{2,0,1:T(1,128)} %copy-done) | copy-start | bytes 5898244
  329.5 82.0 %copy-start.5 = (f32[2560,64]{0,1:T(8,128)S(1)}, f32[2560,64]{0,1:T(8,128)}, u32[]{:S(2)}) copy-start(f32[2560,64]{0,1:T(8,128)} %copy-done.4) | copy-start | bytes 1966084
  414.5 35.9 %all-to-all-start.8 = ((f32[1,64,2560]{2,0,1:T(1,128)}), f32[1,64,2560]{2,0,1:T(1,128)S(1)}, u32[]{:S(2)}, u32[]{:S(2)}) async-start(f32[1,64,2560]{2,0,1:T(1,128)} %copy.32), calls=%async_computation.8 | async-start | bytes 1310720 | tf_op jit(solution)/shard_map/all_to_all | solution.py:133
  450.4 26.4 %all-to-all-start.7 = ((f32[64,1,2560]{2,1,0:T(1,128)}), f32[64,1,2560]{2,1,0:T(1,128)S(1)}, u32[]{:S(2)}, u32[]{:S(2)}) async-start(f32[64,1,2560]{2,1,0:T(1,128)} %copy.31), calls=%async_computation.7 | async-start | bytes 1310720 | tf_op jit(solution)/shard_map/all_to_all | solution.py:137
  476.8 26.4 %all-to-all-start.9 = ((f32[64,1,2560]{2,1,0:T(1,128)}), f32[64,1,2560]{2,1,0:T(1,128)S(1)}, u32[]{:S(2)}, u32[]{:S(2)}) async-start(f32[64,1,2560]{2,1,0:T(1,128)} %copy.33), calls=%async_computation.9 | async-start | bytes 1310720 | tf_op jit(solution)/shard_map/all_to_all | solution.py:138
  (18 other events, 257.6 us)
Sparse Core Ops, SparseCore 0:
  332.1 76.8 all-reduce.2
where the time goes:
time: 521 us; the launch traced here: 511 us
  waiting for transfers between devices  230 us (44%)
  other arithmetic  124 us (24%)
  starting transfers between devices  93.3 us (18%)
  local copies, waits for them, and re-layouts  33.2 us (6%)
  matrix products  15.8 us (3%)
  between operations  15.7 us (3%)
    psum x1, waiting for transfers between devices, on_device(): gram_stiff, gram_plain = lax.psum((gram_stiff, gram_plain), 'elem')  77 us
    add x1, other arithmetic, on_device(): applied + (2.0 * (1.0 - my_cosines))[:, None, None] * span_link * center  66.4 us
    mul x2, other arithmetic, on_device(): rows_all[distance - 1]  48.9 us
    all_to_all x2, waiting for transfers between devices, on_device(): lax.all_to_all(moved[1], 'span', split_axis=0, concat_axis=1, tiled=True)  36.9 us
    all_to_all x2, waiting for transfers between devices, on_device(): lax.all_to_all(moved[0], 'span', split_axis=0, concat_axis=1, tiled=True)  35.4 us
    all_to_all x1, waiting for transfers between devices, on_device(): lax.all_to_all(current_block, 'span', split_axis=1, concat_axis=0, tiled=...  18.6 us
    all_to_all x1, waiting for transfers between devices, on_device(): lax.all_to_all(search_block, 'span', split_axis=1, concat_axis=0, tiled=T...  18.6 us
    all_to_all x1, waiting for transfers between devices, on_device(): lax.all_to_all(previous_block, 'span', split_axis=1, concat_axis=0, tiled...  17.7 us
  transfers between devices with their start and end apart: 15, of which 10 were waited for; matrix products, arithmetic and copies ran while one was open for 33% of the time, Pallas kernels for 0%

commit v1 on v0

v1 whole, which is shorter than its diff:
```python
import functools
import math

import jax
import jax.numpy as jnp
import ml_dtypes
import numpy as np
from jax import lax
from jax.experimental import pallas as pl
from jax.experimental.pallas import tpu as pltpu
from jax.sharding import PartitionSpec as P

REACH = 8
SPANS = 64
M = 64
HALF = 20
PAD = 24
LANES = 128
F32 = jnp.float32
BF16 = jnp.bfloat16
VMEM = pltpu.VMEM


def split_np(matrix):
    high = matrix.astype(np.float32).astype(ml_dtypes.bfloat16)
    low = (matrix - high.astype(np.float64)).astype(ml_dtypes.bfloat16)
    return high, low


def fourier_np(count):
    half = count // 2
    row = np.arange(count)[:, None]
    col = np.arange(count)[None, :]
    wave = np.where(row <= half, row, row - half)
    phase = (wave * col % count) * (2.0 * math.pi / count)
    scaled = np.where(row <= half, np.cos(phase), np.sin(phase)) * math.sqrt(2.0 / count)
    edge = (row == 0) | (row == half)
    matrix = np.where(edge, np.cos(phase) * math.sqrt(1.0 / count), scaled)
    slots = np.arange(count)
    slot_wave = np.where(slots <= half, slots, slots - half)
    links = 2.0 * (1.0 - np.cos(slot_wave * (2.0 * math.pi / count)))
    return matrix, links


def left_terms(matrix):
    high, low = split_np(matrix)
    return np.concatenate([high, low, high], 1)


def split(value):
    high = value.astype(BF16)
    low = (value - high.astype(F32)).astype(BF16)
    return high, low


def right_rows(value):
    high, low = split(value)
    return jnp.concatenate([high, high, low], 0)


def lane_low(shape):
    return lax.broadcasted_iota(jnp.int32, shape, len(shape) - 1) < M


def full(count):
    return [pl.BlockSpec(memory_space=VMEM)] * count


def params(collective=None, limit=56):
    return pltpu.CompilerParams(
        vmem_limit_bytes=limit << 20,
        collective_id=collective,
        has_side_effects=collective is not None,
    )


def pack_kernel(x_ref, w_ref, p_ref, xw_ref, pp_ref):
    dofs = x_ref.shape[1]
    p = p_ref[...]
    moved = pltpu.roll(p, dofs - HALF, 1)
    for block in range(dofs // LANES):
        at = slice(block * LANES, (block + 1) * LANES)
        xw_ref[at, :] = jnp.concatenate([x_ref[:, at], w_ref[:, at]], 0).T
        pp_ref[at, :] = jnp.concatenate([p[:, at], moved[:, at]], 0).T


def arrived(ref, sem):
    pltpu.make_async_copy(ref, ref, sem).wait()


def greet(spans):
    me = lax.axis_index("span")
    barrier = pltpu.get_barrier_semaphore()

    def signal(step, _):
        pl.semaphore_signal(
            barrier,
            inc=1,
            device_id={"span": lax.rem(me + step, spans)},
            device_id_type=pl.DeviceIdType.MESH,
        )
        return 0

    lax.fori_loop(1, spans, signal, 0)
    return barrier


def send(src, dst, send_sem, recv_sem, device):
    copy = pltpu.make_async_remote_copy(
        src_ref=src,
        dst_ref=dst,
        send_sem=send_sem,
        recv_sem=recv_sem,
        device_id=device,
        device_id_type=pl.DeviceIdType.MESH,
    )
    copy.start()
    return copy


def forward_kernel(xw_ref, pp_ref, rot_ref, edge_ref, rxw_ref, rpp_ref, rall_ref, left_ref, sems, rsems):
    spans = SPANS
    me = lax.axis_index("span")
    ex, count_x = me // 16, 4
    ez, count_z = lax.rem(me // 2, 8), 8
    ec = lax.rem(me, 2)
    elem = lax.axis_index("elem")
    elems = lax.axis_size("elem")
    barrier = greet(spans)
    after, before = lax.rem(elem + 1, elems), lax.rem(elem + elems - 1, elems)
    for other in (after, before):
        pl.semaphore_signal(
            barrier, inc=1, device_id={"elem": other}, device_id_type=pl.DeviceIdType.MESH
        )
    own = [
        pltpu.make_async_copy(rot_ref, rall_ref.at[ex, ez, ec], rsems.at[8]),
        pltpu.make_async_copy(xw_ref.at[me], rxw_ref.at[:, me], rsems.at[9]),
        pltpu.make_async_copy(pp_ref.at[2 * me], rpp_ref.at[:, me], rsems.at[10]),
    ]
    for copy in own:
        copy.start()
    pl.semaphore_wait(barrier, spans - 1 + 2)

    def at(x, z, c):
        return {"span": (x * 8 + z) * 2 + c}

    for step in range(1, count_z):
        send(
            rot_ref,
            rall_ref.at[ex, ez, ec],
            rsems.at[0],
            rsems.at[1],
            at(ex, lax.rem(ez + step, count_z), ec),
        )
    edge = send(edge_ref, left_ref, rsems.at[6], rsems.at[7], {"elem": after})

    def body(step, _):
        other = lax.rem(me + step, spans)
        send(xw_ref.at[other], rxw_ref.at[:, me], sems.at[0], sems.at[1], {"span": other})
        send(pp_ref.at[2 * other], rpp_ref.at[:, me], sems.at[2], sems.at[3], {"span": other})
        return 0

    lax.fori_loop(1, spans, body, 0)
    own[0].wait()
    arrived(rall_ref.at[0, pl.ds(0, count_z - 1), 0], rsems.at[1])
    for step in range(1, count_x):
        send(
            rall_ref.at[ex, :, ec],
            rall_ref.at[ex, :, ec],
            rsems.at[2],
            rsems.at[3],
            at(lax.rem(ex + step, count_x), ez, ec),
        )
    arrived(rall_ref.at[pl.ds(0, count_x - 1), :, 0], rsems.at[3])
    cross = send(
        rall_ref.at[:, :, ec], rall_ref.at[:, :, ec], rsems.at[4], rsems.at[5], at(ex, ez, 1 - ec)
    )
    arrived(rall_ref.at[0, pl.ds(0, count_z - 1), 0], rsems.at[0])
    arrived(rall_ref.at[pl.ds(0, count_x - 1), :, 0], rsems.at[2])
    cross.wait()
    edge.wait()
    own[1].wait()
    own[2].wait()
    arrived(rxw_ref.at[:, pl.ds(0, spans - 1)], sems.at[0])
    arrived(rxw_ref.at[:, pl.ds(0, spans - 1)], sems.at[1])
    arrived(rpp_ref.at[:, pl.ds(0, spans - 1)], sems.at[2])
    arrived(rpp_ref.at[:, pl.ds(0, spans - 1)], sems.at[3])


def rotate_kernel(xw_ref, pp_ref, rall_ref, four_ref, out_ref, low_ref, high_ref, slot_ref):
    slot_ref[...] = jnp.zeros_like(slot_ref)
    group = 4

    def transform(source, base, which, start):
        rows = jnp.concatenate([source[base + q] for q in range(group)], 1)
        moved = jnp.dot(four_ref[...], right_rows(rows), preferred_element_type=F32)
        for q in range(group):
            slot_ref[which, pl.ds(start + q, SPANS, stride=PAD), :] = moved[
                :, q * LANES : (q + 1) * LANES
            ]

    def chunk(step, _):
        at = step * group
        transform(xw_ref, at, 0, at)
        transform(xw_ref, at + HALF, 1, at)
        transform(pp_ref, at, 2, at)
        return 0

    lax.fori_loop(0, HALF // group, chunk, 0)
    low = lane_low((96, LANES))

    def slot(j, _):
        at = pl.ds(pl.multiple_of(j * PAD, 8), PAD)
        rows = jnp.concatenate([slot_ref[which, at, :] for which in range(3)], 1)
        high, rest = split(rows)
        left = jnp.concatenate([high, rest, high], 1)
        packed = rall_ref[j]
        turned = pltpu.roll(packed, M, 1)
        a_low, b_low = jnp.where(low, packed, 0.0), jnp.where(low, turned, 0.0)
        a_high, b_high = jnp.where(low, 0.0, turned), jnp.where(low, 0.0, packed)
        right = jnp.concatenate(
            [a_low, b_low[:32], a_high, b_high[:32], b_low[32:], b_high[32:]], 0
        )
        moved = jnp.dot(left, right_rows(right), preferred_element_type=F32)
        out_ref[at, :] = moved
        low_ref[j] = moved[:REACH]
        high_ref[j] = moved[HALF - REACH : HALF]
        return 0

    lax.fori_loop(0, SPANS, slot, 0)


def halo_kernel(low_ref, high_ref, left_ref, right_ref, sems):
    me, elem = lax.axis_index("span"), lax.axis_index("elem")
    spans, elems = lax.axis_size("span"), lax.axis_size("elem")
    up, down = me + 1, me + spans - 1
    after = {"span": lax.rem(up, spans), "elem": lax.rem(elem + up // spans, elems)}
    before = {
        "span": lax.rem(down, spans),
        "elem": lax.rem(elem + elems - 1 + down // spans, elems),
    }
    barrier = pltpu.get_barrier_semaphore()
    for other in (after, before):
        pl.semaphore_signal(barrier, inc=1, device_id=other, device_id_type=pl.DeviceIdType.MESH)
    pl.semaphore_wait(barrier, 2)
    copies = [
        send(high_ref, left_ref, sems.at[0], sems.at[1], after),
        send(low_ref, right_ref, sems.at[2], sems.at[3], before),
    ]
    for copy in copies:
        copy.wait()


def stiff_kernel(p_ref, low_ref, high_ref, left_ref, right_ref, band_ref, link_ref, slots_ref, out_ref, sums_ref):
    group = 4
    half = lane_low((REACH, LANES))
    low = lane_low((PAD, LANES))
    kept = lax.broadcasted_iota(jnp.int32, (PAD, LANES), 0) < HALF
    side = lane_low((1, LANES))
    high, rest = split(band_ref[...])
    band = jnp.concatenate([high, rest, high], 1)

    def body(step, _):
        pieces = []
        for q in range(group):
            j = step * group + q
            rows = p_ref[pl.ds(pl.multiple_of(j * PAD, 8), PAD), :]
            top = pltpu.roll(jnp.where(half, high_ref[j], left_ref[j]), M, 1)
            bottom = pltpu.roll(jnp.where(half, right_ref[j], low_ref[j]), M, 1)
            pieces.append(jnp.concatenate([rows, top, bottom], 0))
        wide = jnp.concatenate(pieces, 1)
        moved = jnp.dot(band, right_rows(wide), preferred_element_type=F32)
        for q in range(group):
            j = step * group + q
            at = slice(q * LANES, (q + 1) * LANES)
            rows = pieces[q][:PAD]
            stiff = jnp.where(low, moved[:PAD, at], moved[PAD:, at])
            stiff = stiff + slots_ref[j] * link_ref[...] * rows
            out_ref[pl.ds(pl.multiple_of(j * PAD, 8), PAD), :] = stiff
            energy = jnp.sum(jnp.where(kept, rows * stiff, 0.0), 0, keepdims=True)
            weight = jnp.sum(jnp.where(kept, rows * rows, 0.0), 0, keepdims=True)
            energy = energy + pltpu.roll(energy, M, 1)
            weight = weight + pltpu.roll(weight, M, 1)
            sums_ref[j] = jnp.where(side, energy, weight)
        return 0

    lax.fori_loop(0, SPANS // group, body, 0)


def ritz_kernel(sums_ref, all_ref, parts_ref, mine_ref, elems_ref, sems):
    spans, elems = SPANS, lax.axis_size("elem")
    me, elem = lax.axis_index("span"), lax.axis_index("elem")
    barrier = greet(spans)
    for step in range(1, elems):
        pl.semaphore_signal(
            barrier,
            inc=1,
            device_id={"elem": lax.rem(elem + step, elems)},
            device_id_type=pl.DeviceIdType.MESH,
        )
    parts_ref[me] = sums_ref[me]
    pl.semaphore_wait(barrier, spans - 1 + elems - 1)

    def scatter(step, _):
        other = lax.rem(me + step, spans)
        send(sums_ref.at[other], parts_ref.at[me], sems.at[0], sems.at[1], {"span": other})
        return 0

    lax.fori_loop(1, spans, scatter, 0)
    arrived(parts_ref.at[pl.ds(0, spans - 1)], sems.at[1])
    mine = jnp.sum(parts_ref[...], 0)
    mine_ref[...] = mine
    elems_ref[elem] = mine
    for step in range(1, elems):
        send(
            mine_ref,
            elems_ref.at[elem],
            sems.at[2],
            sems.at[3],
            {"elem": lax.rem(elem + step, elems)},
        )
    arrived(elems_ref.at[pl.ds(0, elems - 1)], sems.at[3])
    total = jnp.sum(elems_ref[...], 0)
    ritz = total / (pltpu.roll(total, M, 1) + 1e-06)
    ritz = jnp.where(lane_low((1, LANES)), ritz, pltpu.roll(ritz, M, 1))
    all_ref[me] = ritz

    def spread(step, _):
        other = lax.rem(me + step, spans)
        send(all_ref.at[me], all_ref.at[me], sems.at[4], sems.at[5], {"span": other})
        return 0

    lax.fori_loop(1, spans, spread, 0)
    arrived(parts_ref.at[pl.ds(0, spans - 1)], sems.at[0])
    arrived(elems_ref.at[pl.ds(0, elems - 1)], sems.at[2])
    arrived(all_ref.at[pl.ds(0, spans - 1)], sems.at[4])
    arrived(all_ref.at[pl.ds(0, spans - 1)], sems.at[5])


def return_kernel(p_ref, stiff_ref, ritz_ref, four_ref, block_ref, res_ref):
    group = 2

    def body(step, _):
        pieces = []
        for q in range(group):
            rows = pl.ds(step * group + q, SPANS, stride=PAD)
            projected = p_ref[rows, :]
            pieces += [projected, stiff_ref[rows, :] - ritz_ref[...] * projected]
        moved = jnp.dot(
            four_ref[...], right_rows(jnp.concatenate(pieces, 1)), preferred_element_type=F32
        )
        for q in range(group):
            k = step * group + q
            block_ref[k] = moved[:, 2 * q * LANES : (2 * q + 1) * LANES]
            res_ref[k] = moved[:, (2 * q + 1) * LANES : (2 * q + 2) * LANES]
        return 0

    lax.fori_loop(0, HALF // group, body, 0)


def backward_kernel(block_ref, res_ref, got_block_ref, got_res_ref, sems):
    spans = SPANS
    me = lax.axis_index("span")
    barrier = greet(spans)
    own = [
        pltpu.make_async_copy(block_ref.at[:, me], got_block_ref.at[me], sems.at[4]),
        pltpu.make_async_copy(res_ref.at[:, me], got_res_ref.at[me], sems.at[5]),
    ]
    for copy in own:
        copy.start()
    pl.semaphore_wait(barrier, spans - 1)

    def body(step, _):
        other = lax.rem(me + step, spans)
        where = {"span": other}
        send(block_ref.at[:, other], got_block_ref.at[me], sems.at[0], sems.at[1], where)
        send(res_ref.at[:, other], got_res_ref.at[me], sems.at[2], sems.at[3], where)
        return 0

    lax.fori_loop(1, spans, body, 0)
    for copy in own:
        copy.wait()
    arrived(got_block_ref.at[pl.ds(0, spans - 1)], sems.at[0])
    arrived(got_block_ref.at[pl.ds(0, spans - 1)], sems.at[1])
    arrived(got_res_ref.at[pl.ds(0, spans - 1)], sems.at[2])
    arrived(got_res_ref.at[pl.ds(0, spans - 1)], sems.at[3])


def unpack_kernel(block_ref, res_ref, next_ref, out_ref, rows_ref):
    low = lane_low((HALF, LANES))

    def body(i, _):
        block, res = block_ref[i], res_ref[i]
        first = jnp.where(low, block, pltpu.roll(res, M, 1))
        second = jnp.where(low, pltpu.roll(block, M, 1), res)
        rows_ref[pl.ds(pl.multiple_of(i * 2 * HALF, 8), 2 * HALF), :] = jnp.concatenate(
            [first, second], 0
        )
        return 0

    lax.fori_loop(0, SPANS, body, 0)
    for block in range(rows_ref.shape[0] // LANES):
        at = slice(block * LANES, (block + 1) * LANES)
        turned = rows_ref[at, :].T
        next_ref[:, at] = turned[:M]
        out_ref[:, at] = turned[M:]


def shape(*dims):
    return jax.ShapeDtypeStruct(dims, F32)


def band_terms(window, left, first):
    size = 2 * HALF + 2 * REACH
    lane = jnp.arange(size)
    window = jnp.where(first & (lane < REACH), left, window)
    ground, tension, dropper, offset = window[0], window[1], window[2], window[3]
    row, col = lane[:, None], lane[None, :]
    weight = jnp.where(col == row + 1, tension[:, None], 0.0)
    weight = weight + jnp.where(
        col == row + offset.astype(jnp.int32)[:, None], dropper[:, None], 0.0
    )
    both = weight + weight.T
    stiff = jnp.where(row == col, (ground + jnp.sum(both, 1))[:, None], 0.0) - both
    blank = jnp.zeros((HALF, PAD - HALF), F32)
    gap = jnp.zeros((PAD - HALF, PAD + 2 * REACH), F32)
    low, mid, high = REACH, REACH + HALF, REACH + 2 * HALF
    near, far = stiff[low:mid], stiff[mid:high]
    near = jnp.concatenate(
        [near[:, low:mid], blank, near[:, :low], near[:, mid : mid + REACH]], 1
    )
    far = jnp.concatenate([far[:, mid:high], blank, far[:, mid - REACH : mid], far[:, high:]], 1)
    return jnp.concatenate([near, gap, far, gap], 0)


def on_device(
    current_block,
    search_block,
    previous_block,
    ground_spring,
    wire_tension,
    dropper_stiff,
    dropper_offset,
    span_link,
    ritz_rotation,
):
    dofs = current_block.shape[2]
    spans, elems = lax.axis_size("span"), lax.axis_size("elem")
    me, elem = lax.axis_index("span"), lax.axis_index("elem")
    share = dofs // spans
    matrix, links = fourier_np(spans)

    position = elem * dofs + jnp.arange(dofs)
    total = dofs * elems
    tension = jnp.where(position < total - 1, wire_tension, 0.0)
    dropper = jnp.where(position + dropper_offset < total, dropper_stiff, 0.0)
    coefs = jnp.stack([ground_spring, tension, dropper, dropper_offset.astype(F32), span_link])
    edge = jnp.zeros((8, LANES), F32).at[:5, :REACH].set(coefs[:, dofs - REACH :])
    window = lax.dynamic_slice(
        jnp.pad(coefs, ((0, 0), (REACH, REACH))), (0, me * share), (5, share + 2 * REACH)
    )

    xw, pp = pl.pallas_call(
        pack_kernel,
        out_shape=(shape(dofs, LANES), shape(dofs, LANES)),
        in_specs=full(3),
        out_specs=tuple(full(2)),
        compiler_params=params(),
    )(current_block[0], search_block[0], previous_block[0])
    rotation = jnp.concatenate([ritz_rotation[0, :96], ritz_rotation[0, 96:]], 1)

    got_xw, got_pp, rotations, left_edge = pl.pallas_call(
        forward_kernel,
        out_shape=(
            shape(share, spans, 1, LANES),
            shape(HALF, spans, 1, LANES),
            shape(4, 8, 2, 96, LANES),
            shape(8, LANES),
        ),
        in_specs=full(4),
        out_specs=tuple(full(4)),
        scratch_shapes=[pltpu.SemaphoreType.DMA((4,)), pltpu.SemaphoreType.DMA((11,))],
        compiler_params=params(0),
    )(
        xw.reshape(spans, share, 1, LANES),
        pp.reshape(2 * spans, HALF, 1, LANES),
        rotation,
        edge,
    )

    rows = spans * PAD
    projected, low_edge, high_edge = pl.pallas_call(
        rotate_kernel,
        out_shape=(shape(rows, LANES), shape(spans, REACH, LANES), shape(spans, REACH, LANES)),
        in_specs=full(4),
        out_specs=tuple(full(3)),
        scratch_shapes=[pltpu.VMEM((3, rows, LANES), F32)],
        compiler_params=params(),
    )(
        got_xw.reshape(share, spans, LANES),
        got_pp.reshape(HALF, spans, LANES),
        rotations.reshape(spans, 96, LANES),
        jnp.asarray(left_terms(matrix)),
    )

    from_left, from_right = pl.pallas_call(
        halo_kernel,
        out_shape=(shape(spans, REACH, LANES), shape(spans, REACH, LANES)),
        in_specs=full(2),
        out_specs=tuple(full(2)),
        scratch_shapes=[pltpu.SemaphoreType.DMA((4,))],
        compiler_params=params(1),
    )(low_edge, high_edge)

    band = band_terms(window, jnp.pad(left_edge[:5, :REACH], ((0, 0), (0, share + REACH))), me == 0)
    link = window[4, REACH : REACH + share].reshape(2, HALF).T
    link = jnp.pad(jnp.repeat(link, M, 1), ((0, PAD - HALF), (0, 0)))
    slots = jnp.asarray(np.repeat(links[:, None, None], LANES, 2).astype(np.float32))
    stiff, sums = pl.pallas_call(
        stiff_kernel,
        out_shape=(shape(rows, LANES), shape(spans, 1, LANES)),
        in_specs=full(8),
        out_specs=tuple(full(2)),
        compiler_params=params(),
    )(projected, low_edge, high_edge, from_left, from_right, band, link, slots)

    ritz = pl.pallas_call(
        ritz_kernel,
        out_shape=shape(spans, 1, LANES),
        in_specs=full(1),
        out_specs=full(1)[0],
        scratch_shapes=[
            pltpu.VMEM((spans, 1, LANES), F32),
            pltpu.VMEM((1, LANES), F32),
            pltpu.VMEM((elems, 1, LANES), F32),
            pltpu.SemaphoreType.DMA((6,)),
        ],
        compiler_params=params(2),
    )(sums)

    block, res = pl.pallas_call(
        return_kernel,
        out_shape=(shape(HALF, spans, LANES), shape(HALF, spans, LANES)),
        in_specs=full(4),
        out_specs=tuple(full(2)),
        compiler_params=params(),
    )(projected, stiff, ritz.reshape(spans, LANES), jnp.asarray(left_terms(matrix.T)))

    got_block, got_res = pl.pallas_call(
        backward_kernel,
        out_shape=(shape(spans, HALF, 1, LANES), shape(spans, HALF, 1, LANES)),
        in_specs=full(2),
        out_specs=tuple(full(2)),
        scratch_shapes=[pltpu.SemaphoreType.DMA((6,))],
        compiler_params=params(3),
    )(block.reshape(HALF, spans, 1, LANES), res.reshape(HALF, spans, 1, LANES))

    next_block, next_residual = pl.pallas_call(
        unpack_kernel,
        out_shape=(shape(M, dofs), shape(M, dofs)),
        in_specs=full(2),
        out_specs=tuple(full(2)),
        scratch_shapes=[pltpu.VMEM((dofs, LANES), F32)],
        compiler_params=params(),
    )(got_block.reshape(spans, HALF, LANES), got_res.reshape(spans, HALF, LANES))
    mine = lax.dynamic_slice(ritz, (me, 0, 0), (1, 1, M)).reshape(1, M)
    return (next_block[None], next_residual[None], mine)


def solution(mesh):
    return jax.shard_map(
        on_device,
        mesh=mesh,
        in_specs=(
            P("span", None, "elem"),
            P("span", None, "elem"),
            P("span", None, "elem"),
            P("elem"),
            P("elem"),
            P("elem"),
            P("elem"),
            P("elem"),
            P("span", None, None),
        ),
        out_specs=(P("span", None, "elem"), P("span", None, "elem"), P("span", None)),
        check_vma=False,
    )
```

time: 521 us -> 202 us (0.39); the launches traced: 511 us -> 201 us
  waiting for transfers between devices: 230 us -> 0 us
  Pallas kernels: 0 us -> 192 us
  other arithmetic: 124 us -> 1.83 us
  starting transfers between devices: 93.3 us -> 0 us
  local copies, waits for them, and re-layouts: 33.2 us -> 6.54 us
  matrix products: 15.8 us -> 0 us
  between operations: 15.7 us -> 0.89 us
    pallas_call x0 -> x9, Pallas kernels: none -> 192 us  [the longest x1 71.8 us: on_device(): pl.pallas_call(forward_kernel, out_shape=(shape(share, spans, 1, LANES),...]
    all_to_all x10 -> x0, waiting for transfers between devices: 152 us -> none  [the longest x2 36.9 us: on_device(): lax.all_to_all(moved[1], 'span', split_axis=0, concat_axis=1, tiled=True)]
    all_to_all x10 -> x0, starting transfers between devices: 81.5 us -> none  [the longest x1 15.8 us: on_device(): lax.all_to_all(residual, 'span', split_axis=1, concat_axis=0, tiled=True)]
    psum x1 -> x0, waiting for transfers between devices: 77 us -> none  [on_device(): gram_stiff, gram_plain = lax.psum((gram_stiff, gram_plain), 'elem')]
    add x1 -> x3, other arithmetic: 66.4 us -> 0.02 us  [the longest x1 0.01 us: band_terms(): row + offset.astype(jnp.int32)[:, None]]
    mul x4 -> x0, other arithmetic: 53.2 us -> none  [the longest x2 48.9 us: on_device(): rows_all[distance - 1]]
    dot_general x11 -> x0, matrix products: 15.8 us -> none  [the longest x5 5.58 us: along_spans(): return jnp.dot(matrix, flat, precision=lax.Precision.HIGHEST).reshape(shape)]
    concatenate x1 -> x0, local copies, waits for them, and re-layouts: 13.4 us -> none  [with_halo(): jnp.concatenate([lax.ppermute(tail, axis, [(i, (i + 1) % count) for i in...]
  transfers between devices with their start and end apart: 15 -> 0, of which waited for: 10 -> 0; matrix products, arithmetic and copies ran while one was open for 33% -> 0% of each run, Pallas kernels for 0% -> 0%
where the time goes in v1:
time: 202 us; the launch traced here: 201 us
  Pallas kernels  192 us (95%)
  local copies, waits for them, and re-layouts  6.54 us (3%)
    pallas_call x1, Pallas kernels, on_device(): pl.pallas_call(forward_kernel, out_shape=(shape(share, spans, 1, LANES),...  71.8 us
    pallas_call x1, Pallas kernels, on_device(): pl.pallas_call(backward_kernel, out_shape=(shape(spans, HALF, 1, LANES),...  39.1 us
    pallas_call x1, Pallas kernels, on_device(): pl.pallas_call(ritz_kernel, out_shape=shape(spans, 1, LANES), in_specs=fu...  27 us
    pallas_call x1, Pallas kernels, on_device(): pl.pallas_call(rotate_kernel, out_shape=(shape(rows, LANES), shape(spans,...  21 us
    pallas_call x1, Pallas kernels, on_device(): pl.pallas_call(halo_kernel, out_shape=(shape(spans, REACH, LANES), shape(...  10.4 us
    pallas_call x1, Pallas kernels, on_device(): pl.pallas_call(unpack_kernel, out_shape=(shape(M, dofs), shape(M, dofs)),...  7.53 us
    pallas_call x1, Pallas kernels, on_device(): pl.pallas_call(stiff_kernel, out_shape=(shape(rows, LANES), shape(spans,...  7.16 us
    pallas_call x1, Pallas kernels, on_device(): pl.pallas_call(return_kernel, out_shape=(shape(HALF, spans, LANES), shape...  4.2 us

profile of v1, /device:TPU:1, one launch (start us, length us, event | category | flops | bytes accessed | tf_op | source)
XLA Modules:
  0.0 201.4 jit_solution(13488100279893098326)
XLA Ops:
  0.7 4.0 %shard_map.139 = (f32[2560,128]{1,0:T(8,128)}, f32[2560,128]{1,0:T(8,128)}) custom-call(f32[64,2560]{1,0:T(8,128)} %bitcast.44, f32[64,2560]{1,0:T(8,128)} %bitcast.45, f32[64,2560]{1,0:T(8,128)} %bitcast.46), custom_call_target="tpu_custom_call" | custom-call | tf_op jit(solution)/shard_map/pallas_call | solution.py:463
  4.7 0.1 copy.28
  4.8 0.1 copy.27
  4.9 0.7 pad_maximum_fusion.rot_ref
  5.8 0.1 stack.23
  6.0 0.6 scatter.4.edge_ref
  6.6 71.8 %shard_map.140 = (f32[40,64,1,128]{3,2,1,0:T(1,128)}, f32[20,64,1,128]{3,2,1,0:T(1,128)}, f32[4,8,2,96,128]{4,3,2,1,0:T(8,128)}, f32[8,128]{1,0:T(8,128)}) custom-call(f32[64,40,1,128]{3,2,1,0:T(1,128)} %bitcast.39, f32[128,20,1,128]{3,2,1,0:T(1,128)} %bitcast.40, f32[96,128]{1,0:T(8,128)} %pad_maximum_fusion.rot_ref, f32[8,128]{1,0:T(8,128)} %scatter.4.edge_ref), custom_call_target="tpu_custom_call" | custom-call | tf_op jit(solution)/shard_map/pallas_call | solution.py:472
  78.4 21.0 %shard_map.141 = (f32[1536,128]{1,0:T(8,128)}, f32[64,8,128]{2,1,0:T(8,128)}, f32[64,8,128]{2,1,0:T(8,128)}) custom-call(f32[40,64,128]{2,1,0:T(8,128)} %bitcast.38, f32[20,64,128]{2,1,0:T(8,128)} %bitcast.41, f32[64,96,128]{2,1,0:T(8,128)} %bitcast.35, bf16[64,192]{1,0:T(8,128)(2,1)} %constant.64.clone.four_ref), custom_call_target="tpu_custom_call" | custom-call | tf_op jit(solution)/shard_map/pallas_call | solution.py:492
  99.4 10.4 %shard_map.142 = (f32[64,8,128]{2,1,0:T(8,128)}, f32[64,8,128]{2,1,0:T(8,128)}) custom-call(f32[64,8,128]{2,1,0:T(8,128)} %get-tuple-element.40.low_ref, f32[64,8,128]{2,1,0:T(8,128)} %get-tuple-element.41.high_ref), custom_call_target="tpu_custom_call" | custom-call | tf_op jit(solution)/shard_map/pallas_call | solution.py:506
  109.9 0.2 fusion
  110.1 0.1 select_subtract_fusion
  110.4 0.7 pad_maximum_fusion.1.band_ref
  111.1 0.1 slice_reduce_fusion
  111.2 0.1 reshape_squeeze.3
  111.2 0.1 copy.20
  111.5 0.6 pad.20.link_ref
  112.1 7.2 %shard_map.143 = (f32[1536,128]{1,0:T(8,128)}, f32[64,1,128]{2,1,0:T(1,128)}) custom-call(f32[1536,128]{1,0:T(8,128)} %get-tuple-element.39.p_ref, f32[64,8,128]{2,1,0:T(8,128)} %get-tuple-element.40.low_ref, f32[64,8,128]{2,1,0:T(8,128)} %get-tuple-element.41.high_ref, f32[64,8,128]{2,1,0:T(8,128)} %get-tuple-element.42.left_ref, ...), custom_call_target="tpu_custom_call" | custom-call | tf_op jit(solution)/shard_map/pallas_call | solution.py:519
  119.3 27.0 %shard_map.144 = f32[64,1,128]{2,1,0:T(1,128)} custom-call(f32[64,1,128]{2,1,0:T(1,128)} %get-tuple-element.46.sums_ref), custom_call_target="tpu_custom_call" | custom-call | tf_op jit(solution)/shard_map/pallas_call | solution.py:527
  146.3 4.2 %shard_map.145 = (f32[20,64,128]{2,1,0:T(8,128)}, f32[20,64,128]{2,1,0:T(8,128)}) custom-call(f32[1536,128]{1,0:T(8,128)} %get-tuple-element.39.p_ref, f32[1536,128]{1,0:T(8,128)} %get-tuple-element.45.stiff_ref, f32[64,128]{1,0:T(8,128)} %bitcast.49, bf16[64,192]{1,0:T(8,128)(2,1)} %constant.66.clone.four_ref), custom_call_target="tpu_custom_call" | custom-call | tf_op jit(solution)/shard_map/pallas_call | solution.py:541
  150.5 39.1 %shard_map.146 = (f32[64,20,1,128]{3,2,1,0:T(1,128)}, f32[64,20,1,128]{3,2,1,0:T(1,128)}) custom-call(f32[20,64,1,128]{3,2,1,0:T(1,128)} %bitcast.42, f32[20,64,1,128]{3,2,1,0:T(1,128)} %bitcast.43), custom_call_target="tpu_custom_call" | custom-call | tf_op jit(solution)/shard_map/pallas_call | solution.py:549
  189.6 2.1 %copy.32 = f32[64,20,1,128]{3,1,0,2:T(8,128)} copy(f32[64,20,1,128]{3,2,1,0:T(1,128)} %get-tuple-element.49) | data formatting | bytes 1310720 | tf_op jit(solution)/shard_map/reshape | solution.py:565
  191.7 1.0 copy.31
  192.7 7.5 %shard_map.147 = (f32[64,2560]{1,0:T(8,128)}, f32[64,2560]{1,0:T(8,128)}) custom-call(f32[64,20,128]{2,1,0:T(8,128)} %bitcast.36, f32[64,20,128]{2,1,0:T(8,128)} %bitcast.37), custom_call_target="tpu_custom_call" | custom-call | tf_op jit(solution)/shard_map/pallas_call | solution.py:558
  200.2 1.2 dynamic-slice_bitcast_fusion
  (37 shorter events, 0.7 us)
Async XLA Ops:
  0.6 4.0 %copy-start.1 = (f32[1,192,64]{1,2,0:T(8,128)S(1)}, f32[1,192,64]{1,2,0:T(8,128)}, u32[]{:S(2)}) copy-start(f32[1,192,64]{1,2,0:T(8,128)} %param.22) | copy-start | bytes 147460
  0.6 5.0 %copy-start.3 = (f32[2560]{0:T(1024)S(1)}, f32[2560]{0:T(1024)}, u32[]{:S(2)}) copy-start(f32[2560]{0:T(1024)} %param.17) | copy-start | bytes 30724
  0.7 5.0 %copy-start.5 = (f32[2560]{0:T(1024)S(1)}, f32[2560]{0:T(1024)}, u32[]{:S(2)}) copy-start(f32[2560]{0:T(1024)} %param.18) | copy-start | bytes 30724
  0.7 5.0 %copy-start.6 = (f32[2560]{0:T(1024)S(1)}, f32[2560]{0:T(1024)}, u32[]{:S(2)}) copy-start(f32[2560]{0:T(1024)} %param.19) | copy-start | bytes 30724
  0.7 5.0 %copy-start.2 = (s32[2560]{0:T(1024)S(1)}, s32[2560]{0:T(1024)}, u32[]{:S(2)}) copy-start(s32[2560]{0:T(1024)} %param.20) | copy-start | bytes 30724
  0.7 5.1 %copy-start.4 = (f32[2560]{0:T(1024)S(1)}, f32[2560]{0:T(1024)}, u32[]{:S(2)}) copy-start(f32[2560]{0:T(1024)} %param.21) | copy-start | bytes 30724
  78.4 31.4 %copy-start.7 = (f32[8,128]{1,0:T(8,128)S(1)}, f32[8,128]{1,0:T(8,128)}, u32[]{:S(2)}) copy-start(f32[8,128]{1,0:T(8,128)} %get-tuple-element.44) | copy-start | bytes 12292
  189.6 2.1 %copy-start = (f32[64,20,1,128]{3,2,1,0:T(1,128)S(1)}, f32[64,20,1,128]{3,2,1,0:T(1,128)}, u32[]{:S(2)}) copy-start(f32[64,20,1,128]{3,2,1,0:T(1,128)} %get-tuple-element.50) | copy-start | bytes 1966084

commit v2 on v0

v2 whole, which is shorter than its diff:
```python
import functools
import math

import jax
import jax.numpy as jnp
import ml_dtypes
import numpy as np
from jax import lax
from jax.experimental import pallas as pl
from jax.experimental.pallas import tpu as pltpu
from jax.sharding import PartitionSpec as P

REACH = 8
SPANS = 64
M = 64
HALF = 20
PAD = 24
LANES = 128
F32 = jnp.float32
BF16 = jnp.bfloat16
VMEM = pltpu.VMEM


def split_np(matrix):
    high = matrix.astype(np.float32).astype(ml_dtypes.bfloat16)
    low = (matrix - high.astype(np.float64)).astype(ml_dtypes.bfloat16)
    return high, low


def fourier_np(count):
    half = count // 2
    row = np.arange(count)[:, None]
    col = np.arange(count)[None, :]
    wave = np.where(row <= half, row, row - half)
    phase = (wave * col % count) * (2.0 * math.pi / count)
    scaled = np.where(row <= half, np.cos(phase), np.sin(phase)) * math.sqrt(2.0 / count)
    edge = (row == 0) | (row == half)
    matrix = np.where(edge, np.cos(phase) * math.sqrt(1.0 / count), scaled)
    slots = np.arange(count)
    slot_wave = np.where(slots <= half, slots, slots - half)
    links = 2.0 * (1.0 - np.cos(slot_wave * (2.0 * math.pi / count)))
    return matrix, links


def left_terms(matrix):
    high, low = split_np(matrix)
    return np.concatenate([high, low, high], 1)


def split(value):
    high = value.astype(BF16)
    low = (value - high.astype(F32)).astype(BF16)
    return high, low


def right_rows(value):
    high, low = split(value)
    return jnp.concatenate([high, high, low], 0)


def lane_low(shape):
    return lax.broadcasted_iota(jnp.int32, shape, len(shape) - 1) < M


def full(count):
    return [pl.BlockSpec(memory_space=VMEM)] * count


def params(collective=None, limit=56):
    return pltpu.CompilerParams(
        vmem_limit_bytes=limit << 20,
        collective_id=collective,
        has_side_effects=collective is not None,
    )


def arrived(ref, sem):
    pltpu.make_async_copy(ref, ref, sem).wait()


def send(src, dst, send_sem, recv_sem, device):
    copy = pltpu.make_async_remote_copy(
        src_ref=src,
        dst_ref=dst,
        send_sem=send_sem,
        recv_sem=recv_sem,
        device_id=device,
        device_id_type=pl.DeviceIdType.MESH,
    )
    copy.start()
    return copy


def signal(barrier, device):
    pl.semaphore_signal(
        barrier, inc=1, device_id=device, device_id_type=pl.DeviceIdType.MESH
    )


def rotation_rows(packed):
    low = lane_low(packed.shape)
    turned = pltpu.roll(packed, M, 1)
    a_low, b_low = jnp.where(low, packed, 0.0), jnp.where(low, turned, 0.0)
    a_high, b_high = jnp.where(low, 0.0, turned), jnp.where(low, 0.0, packed)
    rows = jnp.concatenate([a_low, b_low[:32], a_high, b_high[:32], b_low[32:], b_high[32:]], 0)
    high, rest = split(rows)
    return jnp.concatenate([high, rest], 0)


def stiff_rows(value):
    high = value.astype(BF16).astype(F32)
    blank = jnp.zeros((8, value.shape[1]), F32)
    return jnp.concatenate([high, high, value - high, blank], 0).astype(BF16)


def stiffness_band(window, stiff_ref, link_ref):
    row = lax.broadcasted_iota(jnp.int32, (LANES, LANES), 0)
    col = lax.broadcasted_iota(jnp.int32, (LANES, LANES), 1)
    far = (row - col).astype(F32)
    weight = jnp.where(row == col + 1, window[1:2], 0.0) + jnp.where(
        far == window[3:4], window[2:3], 0.0
    )
    both = weight + weight.T
    total = jnp.sum(both, 1, keepdims=True)
    stiff_ref[...] = jnp.where(row == col, window[0:1] + total, 0.0) - both
    link = jnp.sum(jnp.where(row == col, window[4:5], 0.0), 1, keepdims=True)
    link_ref[...] = jnp.broadcast_to(link, (LANES, LANES))
    lane = lax.broadcasted_iota(jnp.int32, (PAD, LANES), 1)

    def place(rows, inner, top, bottom):
        out = jnp.where(lane < HALF, pltpu.roll(rows, (LANES - inner) % LANES, 1), 0.0)
        out = jnp.where(
            (lane >= PAD) & (lane < PAD + REACH), pltpu.roll(rows, (LANES + PAD - top) % LANES, 1), out
        )
        at = PAD + REACH
        return jnp.where(
            (lane >= at) & (lane < at + REACH), pltpu.roll(rows, (LANES + at - bottom) % LANES, 1), out
        )

    near = stiff_ref[REACH : REACH + PAD, :]
    other = stiff_ref[REACH + HALF : REACH + HALF + PAD, :]
    near = place(near, REACH, 0, REACH + HALF)
    other = place(other, REACH + HALF, HALF, REACH + 2 * HALF)
    band = jnp.concatenate([near, other], 0)[:, : PAD + 2 * REACH]
    high = band.astype(BF16).astype(F32)
    terms = [high, band - high, high, jnp.zeros((2 * PAD, 8), F32)]
    links = jnp.where(
        lane < M, link_ref[REACH : REACH + PAD, :], link_ref[REACH + HALF : REACH + HALF + PAD, :]
    )
    return jnp.concatenate(terms, 1).astype(BF16), links


def step_kernel(
    x_ref,
    w_ref,
    p_ref,
    rot_ref,
    edge_ref,
    window_ref,
    four_ref,
    back_ref,
    slots_ref,
    next_ref,
    res_ref,
    ritz_ref,
    xw_ref,
    pp_ref,
    rxw_ref,
    rpp_ref,
    rall_ref,
    right_ref,
    slot_ref,
    proj_ref,
    stiff_ref,
    low_ref,
    high_ref,
    left_in_ref,
    right_in_ref,
    edge_in_ref,
    band_ref,
    link_ref,
    back_block_ref,
    back_res_ref,
    got_block_ref,
    got_res_ref,
    sums_ref,
    part_ref,
    all_ref,
    rows_ref,
    sends,
    recvs,
    locals_,
):
    spans, elems = SPANS, lax.axis_size("elem")
    me, elem = lax.axis_index("span"), lax.axis_index("elem")
    ex, ez, ec = me // 16, lax.rem(me // 2, 8), lax.rem(me, 2)
    dofs = x_ref.shape[1]
    share = 2 * HALF

    up, down = me + 1, me + spans - 1
    after = {"span": lax.rem(up, spans), "elem": lax.rem(elem + up // spans, elems)}
    before = {
        "span": lax.rem(down, spans),
        "elem": lax.rem(elem + elems - 1 + down // spans, elems),
    }

    def at(x, z, c):
        return {"span": (x * 8 + z) * 2 + c}

    def elem_at(step):
        return lax.rem(elem + step, elems)

    barrier = pltpu.get_barrier_semaphore()

    def greet(step, _):
        signal(barrier, {"span": lax.rem(me + step, spans)})
        return 0

    lax.fori_loop(1, spans, greet, 0)
    for step in range(1, elems):
        signal(barrier, {"elem": elem_at(step)})
    signal(barrier, after)
    signal(barrier, before)

    p = p_ref[...]
    moved = pltpu.roll(p, dofs - HALF, 1)
    for block in range(dofs // LANES):
        cut = slice(block * LANES, (block + 1) * LANES)
        xw_ref[cut, :] = jnp.concatenate([x_ref[:, cut], w_ref[:, cut]], 0).T
        pp_ref[cut, :] = jnp.concatenate([p[:, cut], moved[:, cut]], 0).T
    slot_ref[...] = jnp.zeros_like(slot_ref)

    pieces = [
        (xw_ref, 0, rxw_ref.at[pl.ds(0, HALF)]),
        (xw_ref, HALF, rxw_ref.at[pl.ds(HALF, HALF)]),
        (pp_ref, 0, rpp_ref),
    ]
    own = [pltpu.make_async_copy(rot_ref, rall_ref.at[ex, ez, ec], locals_.at[3])]
    for number, (src, offset, dst) in enumerate(pieces):
        own.append(
            pltpu.make_async_copy(
                src.at[pl.ds(me * share + offset, HALF)], dst.at[:, me], locals_.at[number]
            )
        )
    for copy in own:
        copy.start()
    pl.semaphore_wait(barrier, spans - 1 + elems - 1 + 2)

    for step in range(1, 8):
        where = at(ex, lax.rem(ez + step, 8), ec)
        send(rot_ref, rall_ref.at[ex, ez, ec], sends.at[3], recvs.at[3], where)
    edge = send(edge_ref, edge_in_ref, sends.at[6], recvs.at[6], {"elem": elem_at(1)})

    def scatter(number):
        src, offset, dst = pieces[number]

        def body(step, _):
            other = lax.rem(me + step, spans)
            send(
                src.at[pl.ds(other * share + offset, HALF)],
                dst.at[:, me],
                sends.at[number],
                recvs.at[number],
                {"span": other},
            )
            return 0

        lax.fori_loop(1, spans, body, 0)

    rest_z, rest_x = rall_ref.at[0, pl.ds(0, 7), 0], rall_ref.at[pl.ds(0, 3), :, 0]
    scatter(0)
    own[0].wait()
    arrived(rest_z, recvs.at[3])
    for step in range(1, 4):
        mine = rall_ref.at[ex, :, ec]
        send(mine, mine, sends.at[4], recvs.at[4], at(lax.rem(ex + step, 4), ez, ec))
    scatter(1)
    scatter(2)
    edge.wait()
    lane8 = lax.broadcasted_iota(jnp.int32, (8, LANES), 1)
    window = jnp.where((lane8 < REACH) & (me == 0), edge_in_ref[...], window_ref[...])
    band, links = stiffness_band(window, band_ref, link_ref)
    arrived(rest_x, recvs.at[4])
    mine = rall_ref.at[:, :, ec]
    cross = send(mine, mine, sends.at[5], recvs.at[5], at(ex, ez, 1 - ec))

    def prepare(core):
        def body(step, _):
            rows = rotation_rows(rall_ref[step // 8, lax.rem(step, 8), core])
            right_ref[2 * step + core] = rows
            return 0

        lax.fori_loop(0, spans // 2, body, 0)

    prepare(ec)

    def transform(number):
        _, _, dst = pieces[number]
        own[1 + number].wait()
        arrived(dst.at[:, pl.ds(0, spans - 1)], recvs.at[number])
        group = 4

        def body(step, _):
            rows = jnp.concatenate([dst[step * group + q] for q in range(group)], 1)
            out = jnp.dot(four_ref[...], right_rows(rows), preferred_element_type=F32)
            for q in range(group):
                slot_ref[number, pl.ds(step * group + q, spans, stride=PAD), :] = out[
                    :, q * LANES : (q + 1) * LANES
                ]
            return 0

        lax.fori_loop(0, HALF // group, body, 0)

    transform(0)
    cross.wait()
    prepare(1 - ec)
    transform(1)
    transform(2)

    def rotate(j, _):
        cut = pl.ds(pl.multiple_of(j * PAD, 8), PAD)
        rows = jnp.concatenate([slot_ref[number, cut, :] for number in range(3)], 1)
        high = rows.astype(BF16).astype(F32)
        left = jnp.concatenate([high, rows - high], 0).astype(BF16)
        out = jnp.dot(
            jnp.concatenate([left, left], 1), right_ref[j], preferred_element_type=F32
        )
        out = out[:PAD] + out[PAD:]
        proj_ref[cut, :] = out
        low_ref[j] = out[:REACH]
        high_ref[j] = out[HALF - REACH : HALF]
        return 0

    lax.fori_loop(0, spans, rotate, 0, unroll=2)
    halo = [
        send(high_ref, left_in_ref, sends.at[7], recvs.at[7], after),
        send(low_ref, right_in_ref, sends.at[8], recvs.at[8], before),
    ]

    def inverse(source, target):
        group = 4

        def body(step, _):
            rows = [source(pl.ds(step * group + q, spans, stride=PAD)) for q in range(group)]
            out = jnp.dot(
                back_ref[...], right_rows(jnp.concatenate(rows, 1)), preferred_element_type=F32
            )
            for q in range(group):
                target[step * group + q] = out[:, q * LANES : (q + 1) * LANES]
            return 0

        lax.fori_loop(0, HALF // group, body, 0)

    def give_back(source, target, number):
        copy = pltpu.make_async_copy(source.at[:, me], target.at[me], locals_.at[number])
        copy.start()

        def body(step, _):
            other = lax.rem(me + step, spans)
            send(
                source.at[:, other],
                target.at[me],
                sends.at[number],
                recvs.at[number],
                {"span": other},
            )
            return 0

        lax.fori_loop(1, spans, body, 0)
        return copy

    inverse(lambda rows: proj_ref[rows, :], back_block_ref)
    own_block = give_back(back_block_ref, got_block_ref, 9)

    for copy in halo:
        copy.wait()
    half = lane_low((REACH, LANES))
    low = lane_low((PAD, LANES))
    kept = lax.broadcasted_iota(jnp.int32, (PAD, LANES), 0) < HALF
    side = lane_low((1, LANES))

    def stiffen(step, _):
        group = 4
        parts = []
        for q in range(group):
            j = step * group + q
            rows = proj_ref[pl.ds(pl.multiple_of(j * PAD, 8), PAD), :]
            top = pltpu.roll(jnp.where(half, high_ref[j], left_in_ref[j]), M, 1)
            bottom = pltpu.roll(jnp.where(half, right_in_ref[j], low_ref[j]), M, 1)
            parts.append(jnp.concatenate([rows, top, bottom], 0))
        out = jnp.dot(
            band, stiff_rows(jnp.concatenate(parts, 1)), preferred_element_type=F32
        )
        for q in range(group):
            j = step * group + q
            cut = slice(q * LANES, (q + 1) * LANES)
            rows = parts[q][:PAD]
            stiff = jnp.where(low, out[:PAD, cut], out[PAD:, cut])
            stiff = stiff + slots_ref[pl.ds(j, 1), :] * links * rows
            stiff_ref[pl.ds(pl.multiple_of(j * PAD, 8), PAD), :] = stiff
            energy = jnp.sum(jnp.where(kept, rows * stiff, 0.0), 0, keepdims=True)
            weight = jnp.sum(jnp.where(kept, rows * rows, 0.0), 0, keepdims=True)
            energy = energy + pltpu.roll(energy, M, 1)
            weight = weight + pltpu.roll(weight, M, 1)
            sums_ref[pl.ds(j, 1), :] = jnp.where(side, energy, weight)
        return 0

    lax.fori_loop(0, spans // 4, stiffen, 0)

    rest = pl.ds(0, 7)
    part_ref[0, elem] = sums_ref[pl.ds(pl.multiple_of(elem * 8, 8), 8), :]
    for step in range(1, elems):
        other = elem_at(step)
        send(
            sums_ref.at[pl.ds(other * 8, 8)],
            part_ref.at[0, elem],
            sends.at[10],
            recvs.at[10],
            {"elem": other},
        )
    arrived(part_ref.at[0, rest], recvs.at[10])
    part_ref[1, ez] = jnp.sum(part_ref[0], 0)
    for step in range(1, 8):
        where = at(ex, lax.rem(ez + step, 8), ec)
        send(part_ref.at[1, ez], part_ref.at[1, ez], sends.at[11], recvs.at[11], where)
    arrived(part_ref.at[1, rest], recvs.at[11])
    pair = ex * 2 + ec
    part_ref[2, pair] = jnp.sum(part_ref[1], 0)
    for step in range(1, 8):
        other = lax.rem(pair + step, 8)
        where = at(other // 2, ez, lax.rem(other, 2))
        send(part_ref.at[2, pair], part_ref.at[2, pair], sends.at[12], recvs.at[12], where)
    arrived(part_ref.at[2, rest], recvs.at[12])
    total = jnp.sum(part_ref[2], 0)
    ritz = total / (pltpu.roll(total, M, 1) + 1e-06)
    ritz = jnp.where(lane_low((8, LANES)), ritz, pltpu.roll(ritz, M, 1))
    all_ref[elem] = ritz
    for step in range(1, elems):
        send(
            all_ref.at[elem], all_ref.at[elem], sends.at[13], recvs.at[13], {"elem": elem_at(step)}
        )
    arrived(all_ref.at[rest], recvs.at[13])
    ritz = jnp.concatenate([all_ref[g] for g in range(8)], 0)
    sums = lax.broadcasted_iota(jnp.int32, ritz.shape, 0) == me
    ritz_ref[...] = jnp.sum(jnp.where(sums, ritz, 0.0), 0, keepdims=True)

    inverse(lambda rows: stiff_ref[rows, :] - ritz * proj_ref[rows, :], back_res_ref)
    own_res = give_back(back_res_ref, got_res_ref, 14)

    def unpack(source, target):
        def body(i, _):
            rows = source[i]
            both = jnp.concatenate([rows, pltpu.roll(rows, M, 1)], 0)
            rows_ref[pl.ds(pl.multiple_of(i * share, 8), share), :] = both
            return 0

        lax.fori_loop(0, spans, body, 0, unroll=4)
        for block in range(dofs // LANES):
            cut = slice(block * LANES, (block + 1) * LANES)
            target[:, cut] = rows_ref[cut, :].T[:M]

    rest = pl.ds(0, spans - 1)
    own_block.wait()
    arrived(got_block_ref.at[rest], recvs.at[9])
    unpack(got_block_ref, next_ref)
    own_res.wait()
    arrived(got_res_ref.at[rest], recvs.at[14])
    unpack(got_res_ref, res_ref)

    for number, (_, _, dst) in enumerate(pieces):
        arrived(dst.at[:, rest], sends.at[number])
    arrived(rest_z, sends.at[3])
    arrived(rest_x, sends.at[4])
    arrived(got_block_ref.at[rest], sends.at[9])
    for stage in range(3):
        arrived(part_ref.at[stage, pl.ds(0, 7)], sends.at[10 + stage])
    arrived(all_ref.at[pl.ds(0, 7)], sends.at[13])
    arrived(got_res_ref.at[rest], sends.at[14])


def shape(*dims):
    return jax.ShapeDtypeStruct(dims, F32)


def on_device(
    current_block,
    search_block,
    previous_block,
    ground_spring,
    wire_tension,
    dropper_stiff,
    dropper_offset,
    span_link,
    ritz_rotation,
):
    dofs = current_block.shape[2]
    spans, elems = lax.axis_size("span"), lax.axis_size("elem")
    me, elem = lax.axis_index("span"), lax.axis_index("elem")
    share = dofs // spans
    matrix, links = fourier_np(spans)

    position = elem * dofs + jnp.arange(dofs)
    total = dofs * elems
    tension = jnp.where(position < total - 1, wire_tension, 0.0)
    dropper = jnp.where(position + dropper_offset < total, dropper_stiff, 0.0)
    coefs = jnp.stack([ground_spring, tension, dropper, dropper_offset.astype(F32), span_link])
    coefs = jnp.pad(coefs, ((0, 3), (REACH, LANES)))
    edge = coefs[:, dofs : dofs + LANES]
    window = lax.dynamic_slice(coefs, (0, me * share), (8, LANES))
    rotation = jnp.concatenate([ritz_rotation[0, :96], ritz_rotation[0, 96:]], 1)
    rows = spans * PAD
    slots = jnp.asarray(np.repeat(links[:, None], LANES, 1).astype(np.float32))

    next_block, next_residual, ritz = pl.pallas_call(
        step_kernel,
        out_shape=(shape(M, dofs), shape(M, dofs), shape(1, LANES)),
        in_specs=full(9),
        out_specs=tuple(full(3)),
        scratch_shapes=[
            VMEM((dofs, LANES), F32),
            VMEM((dofs, LANES), F32),
            VMEM((share, spans, LANES), F32),
            VMEM((HALF, spans, LANES), F32),
            VMEM((4, 8, 2, 96, LANES), F32),
            VMEM((spans, 768, LANES), BF16),
            VMEM((3, rows, LANES), F32),
            VMEM((rows, LANES), F32),
            VMEM((rows, LANES), F32),
            VMEM((spans, REACH, LANES), F32),
            VMEM((spans, REACH, LANES), F32),
            VMEM((spans, REACH, LANES), F32),
            VMEM((spans, REACH, LANES), F32),
            VMEM((8, LANES), F32),
            VMEM((LANES, LANES), F32),
            VMEM((LANES, LANES), F32),
            VMEM((HALF, spans, LANES), F32),
            VMEM((HALF, spans, LANES), F32),
            VMEM((spans, HALF, LANES), F32),
            VMEM((spans, HALF, LANES), F32),
            VMEM((spans, LANES), F32),
            VMEM((3, 8, 8, LANES), F32),
            VMEM((8, 8, LANES), F32),
            VMEM((dofs, LANES), F32),
            pltpu.SemaphoreType.DMA((15,)),
            pltpu.SemaphoreType.DMA((15,)),
            pltpu.SemaphoreType.DMA((15,)),
        ],
        compiler_params=params(0),
    )(
        current_block[0],
        search_block[0],
        previous_block[0],
        rotation,
        edge,
        window,
        jnp.asarray(left_terms(matrix)),
        jnp.asarray(left_terms(matrix.T)),
        slots,
    )
    return (next_block[None], next_residual[None], ritz[:, :M])


def solution(mesh):
    return jax.shard_map(
        on_device,
        mesh=mesh,
        in_specs=(
            P("span", None, "elem"),
            P("span", None, "elem"),
            P("span", None, "elem"),
            P("elem"),
            P("elem"),
            P("elem"),
            P("elem"),
            P("elem"),
            P("span", None, None),
        ),
        out_specs=(P("span", None, "elem"), P("span", None, "elem"), P("span", None)),
        check_vma=False,
    )
```

time: 521 us -> 143 us (0.27); the launches traced: 511 us -> 143 us
  waiting for transfers between devices: 230 us -> 0 us
  Pallas kernels: 0 us -> 135 us
  other arithmetic: 124 us -> 0.72 us
  starting transfers between devices: 93.3 us -> 0 us
  local copies, waits for them, and re-layouts: 33.2 us -> 6.68 us
  matrix products: 15.8 us -> 0 us
  between operations: 15.7 us -> 0.74 us
    all_to_all x10 -> x0, waiting for transfers between devices: 152 us -> none  [the longest x2 36.9 us: on_device(): lax.all_to_all(moved[1], 'span', split_axis=0, concat_axis=1, tiled=True)]
    pallas_call x0 -> x1, Pallas kernels: none -> 135 us  [on_device(): pl.pallas_call(step_kernel, out_shape=(shape(M, dofs), shape(M, dofs), sh...]
    all_to_all x10 -> x0, starting transfers between devices: 81.5 us -> none  [the longest x1 15.8 us: on_device(): lax.all_to_all(residual, 'span', split_axis=1, concat_axis=0, tiled=True)]
    psum x1 -> x0, waiting for transfers between devices: 77 us -> none  [on_device(): gram_stiff, gram_plain = lax.psum((gram_stiff, gram_plain), 'elem')]
    add x1 -> x0, other arithmetic: 66.4 us -> none  [on_device(): applied + (2.0 * (1.0 - my_cosines))[:, None, None] * span_link * center]
    mul x4 -> x0, other arithmetic: 53.2 us -> none  [the longest x2 48.9 us: on_device(): rows_all[distance - 1]]
    dot_general x11 -> x0, matrix products: 15.8 us -> none  [the longest x5 5.58 us: along_spans(): return jnp.dot(matrix, flat, precision=lax.Precision.HIGHEST).reshape(shape)]
    concatenate x1 -> x0, local copies, waits for them, and re-layouts: 13.4 us -> none  [with_halo(): jnp.concatenate([lax.ppermute(tail, axis, [(i, (i + 1) % count) for i in...]
  transfers between devices with their start and end apart: 15 -> 0, of which waited for: 10 -> 0; matrix products, arithmetic and copies ran while one was open for 33% -> 0% of each run, Pallas kernels for 0% -> 0%
where the time goes in v2:
time: 143 us
  Pallas kernels  135 us (94%)
  local copies, waits for them, and re-layouts  6.68 us (5%)
    pallas_call x1, Pallas kernels, on_device(): pl.pallas_call(step_kernel, out_shape=(shape(M, dofs), shape(M, dofs), sh...  135 us
    unnamed x21, local copies, waits for them, and re-layouts  5.8 us

profile of v2, /device:TPU:1, one launch (start us, length us, event | category | flops | bytes accessed | tf_op | source)
XLA Modules:
  0.0 142.7 jit_solution(9580456987736003839)
XLA Ops:
  0.6 0.0 copy-start.3
  0.6 0.0 copy-start.4
  0.7 0.7 copy-done.3
  1.4 0.0 copy-done.4
  1.4 0.0 copy-start.2
  1.4 0.7 copy-done.2
  2.1 0.0 copy-start.6
  2.1 0.7 copy-done.6
  2.8 0.0 copy-done.5
  2.8 0.1 stack.23
  2.9 0.0 copy-start.1
  2.9 0.7 pad_dynamic-slice_fusion
  3.6 0.2 copy-done.1
  3.8 0.1 fusion.3
  3.8 0.1 copy.17
  3.9 0.1 copy.18
  4.0 0.7 pad_maximum_fusion.rot_ref
  4.7 134.6 %shard_map.139 = (f32[64,2560]{1,0:T(8,128)}, f32[64,2560]{1,0:T(8,128)}, f32[1,128]{1,0:T(1,128)}) custom-call(f32[64,2560]{1,0:T(8,128)} %bitcast.8, f32[64,2560]{1,0:T(8,128)} %bitcast.9, f32[64,2560]{1,0:T(8,128)} %bitcast.10, f32[96,128]{1,0:T(8,128)} %pad_maximum_fusion.rot_ref, f32[8,128]{1,0:T(8,128)} %get-tuple-element.10.edge_ref, ...), custom_call_target="tpu_custom_call" | custom-call | tf_op jit(solution)/shard_map/pallas_call | solution.py:514
  139.3 0.0 copy-start
  139.3 2.0 %copy.22 = f32[1,64,2560]{2,1,0:T(8,128)} copy(f32[1,64,2560]{2,1,0:T(8,128)} %bitcast.12) | data formatting | bytes 1310720
  141.3 0.0 copy-done
  141.4 0.8 copy.23
  142.2 0.0 copy-done.7
  142.2 0.5 copy.24
  (9 shorter events, 0.1 us)
Async XLA Ops:
  0.6 0.7 copy-start.3
  0.6 0.7 copy-start.4
  1.4 0.7 copy-start.2
  2.1 0.7 copy-start.6
  2.1 0.7 copy-start.5
  2.9 0.8 copy-start.1
  139.3 2.0 %copy-start = (f32[64,2560]{1,0:T(8,128)S(1)}, f32[64,2560]{1,0:T(8,128)}, u32[]{:S(2)}) copy-start(f32[64,2560]{1,0:T(8,128)} %get-tuple-element.7) | copy-start | bytes 1966084
  141.4 0.8 copy-start.7

commit v3 on v2

--- a/solution.py
+++ b/solution.py
@@ -117,13 +117,13 @@
     row = lax.broadcasted_iota(jnp.int32, (LANES, LANES), 0)
     col = lax.broadcasted_iota(jnp.int32, (LANES, LANES), 1)
     far = (row - col).astype(F32)
-    weight = jnp.where(row == col + 1, window[1:2], 0.0) + jnp.where(
-        far == window[3:4], window[2:3], 0.0
+    weight = jnp.where(row == col + 1, window[1], 0.0) + jnp.where(
+        far == window[3], window[2], 0.0
     )
     both = weight + weight.T
     total = jnp.sum(both, 1, keepdims=True)
-    stiff_ref[...] = jnp.where(row == col, window[0:1] + total, 0.0) - both
-    link = jnp.sum(jnp.where(row == col, window[4:5], 0.0), 1, keepdims=True)
+    stiff_ref[...] = jnp.where(row == col, window[0] + total, 0.0) - both
+    link = jnp.sum(jnp.where(row == col, window[4], 0.0), 1, keepdims=True)
     link_ref[...] = jnp.broadcast_to(link, (LANES, LANES))
     lane = lax.broadcasted_iota(jnp.int32, (PAD, LANES), 1)
 
@@ -150,23 +150,44 @@
     return jnp.concatenate(terms, 1).astype(BF16), links
 
 
+def unpack(source, rows_ref, target):
+    share = 2 * HALF
+
+    def body(i, _):
+        rows = source[i]
+        both = jnp.concatenate([rows, pltpu.roll(rows, M, 1)], 0)
+        rows_ref[pl.ds(pl.multiple_of(i * share, 8), share), :] = both
+        return 0
+
+    lax.fori_loop(0, SPANS, body, 0, unroll=8)
+    for block in range(rows_ref.shape[0] // LANES):
+        cut = slice(block * LANES, (block + 1) * LANES)
+        target[:, cut] = rows_ref[cut, :].T[:M]
+
+
+def finish_kernel(block_ref, got_ref, next_ref, res_ref, rows_ref):
+    next_ref[...] = block_ref[...]
+    unpack(got_ref, rows_ref, res_ref)
+
+
 def step_kernel(
     x_ref,
     w_ref,
     p_ref,
-    rot_ref,
-    edge_ref,
-    window_ref,
+    coefs_refs,
+    offset_ref,
+    turned_ref,
     four_ref,
     back_ref,
     slots_ref,
     next_ref,
-    res_ref,
+    got_res_ref,
     ritz_ref,
-    xw_ref,
-    pp_ref,
-    rxw_ref,
-    rpp_ref,
+    pack_ref,
+    got_ref,
+    coef_ref,
+    edge_ref,
+    rot_ref,
     rall_ref,
     right_ref,
     slot_ref,
@@ -182,7 +203,6 @@
     back_block_ref,
     back_res_ref,
     got_block_ref,
-    got_res_ref,
     sums_ref,
     part_ref,
     all_ref,
@@ -222,63 +242,96 @@
     signal(barrier, after)
     signal(barrier, before)
 
-    p = p_ref[...]
-    moved = pltpu.roll(p, dofs - HALF, 1)
-    for block in range(dofs // LANES):
-        cut = slice(block * LANES, (block + 1) * LANES)
-        xw_ref[cut, :] = jnp.concatenate([x_ref[:, cut], w_ref[:, cut]], 0).T
-        pp_ref[cut, :] = jnp.concatenate([p[:, cut], moved[:, cut]], 0).T
-    slot_ref[...] = jnp.zeros_like(slot_ref)
-
-    pieces = [
-        (xw_ref, 0, rxw_ref.at[pl.ds(0, HALF)]),
-        (xw_ref, HALF, rxw_ref.at[pl.ds(HALF, HALF)]),
-        (pp_ref, 0, rpp_ref),
-    ]
-    own = [pltpu.make_async_copy(rot_ref, rall_ref.at[ex, ez, ec], locals_.at[3])]
-    for number, (src, offset, dst) in enumerate(pieces):
-        own.append(
-            pltpu.make_async_copy(
-                src.at[pl.ds(me * share + offset, HALF)], dst.at[:, me], locals_.at[number]
-            )
-        )
-    for copy in own:
-        copy.start()
+    rot_ref[...] = jnp.concatenate([turned_ref[:, :96], turned_ref[:, 96:]], 0).T
+    own_rot = pltpu.make_async_copy(rot_ref, rall_ref.at[ex, ez, ec], locals_.at[3])
+    own_rot.start()
     pl.semaphore_wait(barrier, spans - 1 + elems - 1 + 2)
-
     for step in range(1, 8):
         where = at(ex, lax.rem(ez + step, 8), ec)
         send(rot_ref, rall_ref.at[ex, ez, ec], sends.at[3], recvs.at[3], where)
-    edge = send(edge_ref, edge_in_ref, sends.at[6], recvs.at[6], {"elem": elem_at(1)})
-
-    def scatter(number):
-        src, offset, dst = pieces[number]
-
-        def body(step, _):
-            other = lax.rem(me + step, spans)
-            send(
-                src.at[pl.ds(other * share + offset, HALF)],
-                dst.at[:, me],
-                sends.at[number],
-                recvs.at[number],
-                {"span": other},
-            )
+
+    count = dofs // LANES
+    for block in range(count):
+        cut = slice(block * LANES, (block + 1) * LANES)
+        pack_ref[cut, :] = jnp.concatenate([x_ref[:, cut], w_ref[:, cut]], 0).T
+
+    def packed_at(device, number):
+        row = device * share + (number % 2) * HALF + (number // 2) * dofs
+        return pack_ref.at[pl.ds(row, HALF)]
+
+    def message(q):
+        number, step = q // (spans - 1), lax.rem(q, spans - 1) + 1
+        other = lax.rem(me + step, spans)
+        send(
+            packed_at(other, number),
+            got_ref.at[pl.ds(number * HALF, HALF), me],
+            sends.at[number],
+            recvs.at[number],
+            {"span": other},
+        )
+
+    def messages(first, last):
+        def body(q, _):
+            message(q)
             return 0
 
-        lax.fori_loop(1, spans, body, 0)
+        lax.fori_loop(first, last, body, 0)
 
     rest_z, rest_x = rall_ref.at[0, pl.ds(0, 7), 0], rall_ref.at[pl.ds(0, 3), :, 0]
-    scatter(0)
-    own[0].wait()
+    rest_c = rall_ref.at[:, :, 0]
+    messages(0, spans - 1)
+    own_rot.wait()
     arrived(rest_z, recvs.at[3])
     for step in range(1, 4):
         mine = rall_ref.at[ex, :, ec]
         send(mine, mine, sends.at[4], recvs.at[4], at(lax.rem(ex + step, 4), ez, ec))
-    scatter(1)
-    scatter(2)
+    messages(spans - 1, 2 * (spans - 1))
+    p = p_ref[...]
+    moved = pltpu.roll(p, dofs - HALF, 1)
+    for block in range(count):
+        cut = slice(block * LANES, (block + 1) * LANES)
+        below = slice(dofs + block * LANES, dofs + (block + 1) * LANES)
+        pack_ref[below, :] = jnp.concatenate([p[:, cut], moved[:, cut]], 0).T
+    messages(2 * (spans - 1), 3 * (spans - 1))
+    own = []
+    for number in range(3):
+        target = got_ref.at[pl.ds(number * HALF, HALF), me]
+        own.append(pltpu.make_async_copy(packed_at(me, number), target, locals_.at[number]))
+        own[number].start()
+
+    ground_ref, tension_ref, dropper_ref, link_in_ref = coefs_refs
+    grid = (count, LANES)
+    position = elem * dofs + LANES * lax.broadcasted_iota(jnp.int32, grid, 0)
+    position = position + lax.broadcasted_iota(jnp.int32, grid, 1)
+    offset = offset_ref[...]
+    values = [
+        ground_ref[...],
+        jnp.where(position < dofs * elems - 1, tension_ref[...], 0.0),
+        jnp.where(position + offset < dofs * elems, dropper_ref[...], 0.0),
+        offset.astype(F32),
+        link_in_ref[...],
+    ]
+    coef_ref[...] = jnp.zeros_like(coef_ref)
+    edge_ref[...] = jnp.zeros_like(edge_ref)
+    for number, value in enumerate(values):
+        coef_ref[number, 1 : 1 + count, :] = value
+        edge_ref[number : number + 1, :] = value[count - 1 :]
+    edge = send(edge_ref, edge_in_ref, sends.at[6], recvs.at[6], {"elem": elem_at(1)})
+
+    slot_ref[...] = jnp.zeros_like(slot_ref)
+
     edge.wait()
-    lane8 = lax.broadcasted_iota(jnp.int32, (8, LANES), 1)
-    window = jnp.where((lane8 < REACH) & (me == 0), edge_in_ref[...], window_ref[...])
+    for number in range(5):
+        coef_ref[number, 0:1, :] = edge_in_ref[number : number + 1, :]
+    start = LANES - REACH + me * share
+    row, kept_lanes = start // LANES, LANES - lax.rem(start, LANES)
+    turn = lax.rem(kept_lanes, LANES)
+    lane = lax.broadcasted_iota(jnp.int32, (1, LANES), 1)
+    window = []
+    for number in range(5):
+        one = pltpu.roll(coef_ref[number, pl.ds(row, 1), :], turn, 1)
+        two = pltpu.roll(coef_ref[number, pl.ds(row + 1, 1), :], turn, 1)
+        window.append(jnp.where(lane < kept_lanes, one, two))
     band, links = stiffness_band(window, band_ref, link_ref)
     arrived(rest_x, recvs.at[4])
     mine = rall_ref.at[:, :, ec]
@@ -290,18 +343,19 @@
             right_ref[2 * step + core] = rows
             return 0
 
-        lax.fori_loop(0, spans // 2, body, 0)
+        lax.fori_loop(0, spans // 2, body, 0, unroll=4)
 
     prepare(ec)
 
     def transform(number):
-        _, _, dst = pieces[number]
-        own[1 + number].wait()
-        arrived(dst.at[:, pl.ds(0, spans - 1)], recvs.at[number])
+        own[number].wait()
+        arrived(got_ref.at[pl.ds(0, HALF), pl.ds(0, spans - 1)], recvs.at[number])
         group = 4
 
         def body(step, _):
-            rows = jnp.concatenate([dst[step * group + q] for q in range(group)], 1)
+            rows = jnp.concatenate(
+                [got_ref[number * HALF + step * group + q] for q in range(group)], 1
+            )
             out = jnp.dot(four_ref[...], right_rows(rows), preferred_element_type=F32)
             for q in range(group):
                 slot_ref[number, pl.ds(step * group + q, spans, stride=PAD), :] = out[
@@ -309,15 +363,14 @@
                 ]
             return 0
 
-        lax.fori_loop(0, HALF // group, body, 0)
+        lax.fori_loop(0, HALF // group, body, 0, unroll=5)
 
     transform(0)
-    cross.wait()
-    prepare(1 - ec)
     transform(1)
     transform(2)
 
-    def rotate(j, _):
+    def rotate(step, _, core):
+        j = 2 * step + core
         cut = pl.ds(pl.multiple_of(j * PAD, 8), PAD)
         rows = jnp.concatenate([slot_ref[number, cut, :] for number in range(3)], 1)
         high = rows.astype(BF16).astype(F32)
@@ -331,7 +384,10 @@
         high_ref[j] = out[HALF - REACH : HALF]
         return 0
 
-    lax.fori_loop(0, spans, rotate, 0, unroll=2)
+    lax.fori_loop(0, spans // 2, functools.partial(rotate, core=ec), 0, unroll=4)
+    cross.wait_recv()
+    prepare(1 - ec)
+    lax.fori_loop(0, spans // 2, functools.partial(rotate, core=1 - ec), 0, unroll=4)
     halo = [
         send(high_ref, left_in_ref, sends.at[7], recvs.at[7], after),
         send(low_ref, right_in_ref, sends.at[8], recvs.at[8], before),
@@ -349,12 +405,9 @@
                 target[step * group + q] = out[:, q * LANES : (q + 1) * LANES]
             return 0
 
-        lax.fori_loop(0, HALF // group, body, 0)
-
-    def give_back(source, target, number):
-        copy = pltpu.make_async_copy(source.at[:, me], target.at[me], locals_.at[number])
-        copy.start()
-
+        lax.fori_loop(0, HALF // group, body, 0, unroll=5)
+
+    def give_back(source, target, number, first, last):
         def body(step, _):
             other = lax.rem(me + step, spans)
             send(
@@ -366,11 +419,17 @@
             )
             return 0
 
-        lax.fori_loop(1, spans, body, 0)
-        return copy
+        lax.fori_loop(first, last, body, 0)
+
+    def give_block(first, last):
+        give_back(back_block_ref, got_block_ref, 9, first, last)
 
     inverse(lambda rows: proj_ref[rows, :], back_block_ref)
-    own_block = give_back(back_block_ref, got_block_ref, 9)
+    own_block = pltpu.make_async_copy(
+        back_block_ref.at[:, me], got_block_ref.at[me], locals_.at[9]
+    )
+    own_block.start()
+    give_block(1, 25)
 
     for copy in halo:
         copy.wait()
@@ -405,7 +464,7 @@
             sums_ref[pl.ds(j, 1), :] = jnp.where(side, energy, weight)
         return 0
 
-    lax.fori_loop(0, spans // 4, stiffen, 0)
+    lax.fori_loop(0, spans // 4, stiffen, 0, unroll=4)
 
     rest = pl.ds(0, 7)
     part_ref[0, elem] = sums_ref[pl.ds(pl.multiple_of(elem * 8, 8), 8), :]
@@ -418,11 +477,13 @@
             recvs.at[10],
             {"elem": other},
         )
+    give_block(25, 38)
     arrived(part_ref.at[0, rest], recvs.at[10])
     part_ref[1, ez] = jnp.sum(part_ref[0], 0)
     for step in range(1, 8):
         where = at(ex, lax.rem(ez + step, 8), ec)
         send(part_ref.at[1, ez], part_ref.at[1, ez], sends.at[11], recvs.at[11], where)
+    give_block(38, 51)
     arrived(part_ref.at[1, rest], recvs.at[11])
     pair = ex * 2 + ec
     part_ref[2, pair] = jnp.sum(part_ref[1], 0)
@@ -430,6 +491,7 @@
         other = lax.rem(pair + step, 8)
         where = at(other // 2, ez, lax.rem(other, 2))
         send(part_ref.at[2, pair], part_ref.at[2, pair], sends.at[12], recvs.at[12], where)
+    give_block(51, 64)
     arrived(part_ref.at[2, rest], recvs.at[12])
     total = jnp.sum(part_ref[2], 0)
     ritz = total / (pltpu.roll(total, M, 1) + 1e-06)
@@ -445,32 +507,22 @@
     ritz_ref[...] = jnp.sum(jnp.where(sums, ritz, 0.0), 0, keepdims=True)
 
     inverse(lambda rows: stiff_ref[rows, :] - ritz * proj_ref[rows, :], back_res_ref)
-    own_res = give_back(back_res_ref, got_res_ref, 14)
-
-    def unpack(source, target):
-        def body(i, _):
-            rows = source[i]
-            both = jnp.concatenate([rows, pltpu.roll(rows, M, 1)], 0)
-            rows_ref[pl.ds(pl.multiple_of(i * share, 8), share), :] = both
-            return 0
-
-        lax.fori_loop(0, spans, body, 0, unroll=4)
-        for block in range(dofs // LANES):
-            cut = slice(block * LANES, (block + 1) * LANES)
-            target[:, cut] = rows_ref[cut, :].T[:M]
+    own_res = pltpu.make_async_copy(back_res_ref.at[:, me], got_res_ref.at[me], locals_.at[14])
+    own_res.start()
+    give_back(back_res_ref, got_res_ref, 14, 1, spans)
 
     rest = pl.ds(0, spans - 1)
     own_block.wait()
     arrived(got_block_ref.at[rest], recvs.at[9])
-    unpack(got_block_ref, next_ref)
+    unpack(got_block_ref, rows_ref, next_ref)
     own_res.wait()
     arrived(got_res_ref.at[rest], recvs.at[14])
-    unpack(got_res_ref, res_ref)
-
-    for number, (_, _, dst) in enumerate(pieces):
-        arrived(dst.at[:, rest], sends.at[number])
+
+    for number in range(3):
+        arrived(got_ref.at[pl.ds(0, HALF), rest], sends.at[number])
     arrived(rest_z, sends.at[3])
     arrived(rest_x, sends.at[4])
+    arrived(rest_c, sends.at[5])
     arrived(got_block_ref.at[rest], sends.at[9])
     for stage in range(3):
         arrived(part_ref.at[stage, pl.ds(0, 7)], sends.at[10 + stage])
@@ -494,33 +546,25 @@
     ritz_rotation,
 ):
     dofs = current_block.shape[2]
-    spans, elems = lax.axis_size("span"), lax.axis_size("elem")
-    me, elem = lax.axis_index("span"), lax.axis_index("elem")
+    spans = lax.axis_size("span")
     share = dofs // spans
     matrix, links = fourier_np(spans)
 
-    position = elem * dofs + jnp.arange(dofs)
-    total = dofs * elems
-    tension = jnp.where(position < total - 1, wire_tension, 0.0)
-    dropper = jnp.where(position + dropper_offset < total, dropper_stiff, 0.0)
-    coefs = jnp.stack([ground_spring, tension, dropper, dropper_offset.astype(F32), span_link])
-    coefs = jnp.pad(coefs, ((0, 3), (REACH, LANES)))
-    edge = coefs[:, dofs : dofs + LANES]
-    window = lax.dynamic_slice(coefs, (0, me * share), (8, LANES))
-    rotation = jnp.concatenate([ritz_rotation[0, :96], ritz_rotation[0, 96:]], 1)
+    grid = (dofs // LANES, LANES)
     rows = spans * PAD
     slots = jnp.asarray(np.repeat(links[:, None], LANES, 1).astype(np.float32))
 
-    next_block, next_residual, ritz = pl.pallas_call(
+    block, got, ritz = pl.pallas_call(
         step_kernel,
-        out_shape=(shape(M, dofs), shape(M, dofs), shape(1, LANES)),
-        in_specs=full(9),
+        out_shape=(shape(M, dofs), shape(spans, HALF, LANES), shape(1, LANES)),
+        in_specs=full(3) + [full(4)] + full(5),
         out_specs=tuple(full(3)),
         scratch_shapes=[
-            VMEM((dofs, LANES), F32),
-            VMEM((dofs, LANES), F32),
-            VMEM((share, spans, LANES), F32),
-            VMEM((HALF, spans, LANES), F32),
+            VMEM((2 * dofs, LANES), F32),
+            VMEM((3 * HALF, spans, LANES), F32),
+            VMEM((5, 24, LANES), F32),
+            VMEM((8, LANES), F32),
+            VMEM((96, LANES), F32),
             VMEM((4, 8, 2, 96, LANES), F32),
             VMEM((spans, 768, LANES), BF16),
             VMEM((3, rows, LANES), F32),
@@ -536,7 +580,6 @@
             VMEM((HALF, spans, LANES), F32),
             VMEM((HALF, spans, LANES), F32),
             VMEM((spans, HALF, LANES), F32),
-            VMEM((spans, HALF, LANES), F32),
             VMEM((spans, LANES), F32),
             VMEM((3, 8, 8, LANES), F32),
             VMEM((8, 8, LANES), F32),
@@ -550,13 +593,24 @@
         current_block[0],
         search_block[0],
         previous_block[0],
-        rotation,
-        edge,
-        window,
+        [
+            coef.reshape(grid)
+            for coef in (ground_spring, wire_tension, dropper_stiff, span_link)
+        ],
+        dropper_offset.reshape(grid),
+        ritz_rotation[0].T,
         jnp.asarray(left_terms(matrix)),
         jnp.asarray(left_terms(matrix.T)),
         slots,
     )
+    next_block, next_residual = pl.pallas_call(
+        finish_kernel,
+        out_shape=(shape(M, dofs), shape(M, dofs)),
+        in_specs=full(2),
+        out_specs=tuple(full(2)),
+        scratch_shapes=[VMEM((dofs, LANES), F32)],
+        compiler_params=params(limit=16),
+    )(block, got)
     return (next_block[None], next_residual[None], ritz[:, :M])
 
 

time: 143 us -> 129 us (0.902)
  Pallas kernels: 135 us -> 125 us
  local copies, waits for them, and re-layouts: 6.68 us -> 3.35 us
    pallas_call x1 -> x2, Pallas kernels: 135 us -> 125 us  [the longest x1 123 us: on_device(): pl.pallas_call(step_kernel, out_shape=(shape(M, dofs), shape(spans, HALF,...]
    unnamed x21 -> x7, local copies, waits for them, and re-layouts: 5.8 us -> 3.35 us
where the time goes in v3:
time: 129 us
  Pallas kernels  125 us (97%)
  local copies, waits for them, and re-layouts  3.35 us (3%)
    pallas_call x1, Pallas kernels, on_device(): pl.pallas_call(step_kernel, out_shape=(shape(M, dofs), shape(spans, HALF,...  123 us
    unnamed x7, local copies, waits for them, and re-layouts  3.35 us

profile of v3, /device:TPU:1, one launch (start us, length us, event | category | flops | bytes accessed | tf_op | source)
XLA Modules:
  0.0 128.7 jit_solution(250368669427398890)
XLA Ops:
  0.6 122.6 %shard_map.139 = (f32[64,2560]{1,0:T(8,128)}, f32[64,20,128]{2,1,0:T(8,128)}, f32[1,128]{1,0:T(1,128)}) custom-call(f32[64,2560]{1,0:T(8,128)} %bitcast.14, f32[64,2560]{1,0:T(8,128)} %bitcast.15, f32[64,2560]{1,0:T(8,128)} %bitcast.16, f32[20,128]{1,0:T(8,128)} %bitcast.18, f32[20,128]{1,0:T(8,128)} %bitcast.19, f32[20,128]{1,0:T(8,128)} %bitcast.20, ...), custom_call_target="tpu_custom_call" | custom-call | tf_op jit(solution)/shard_map/pallas_call | solution.py:557
  123.3 0.0 copy-start
  123.3 1.1 copy-done
  124.4 0.0 copy-start.1
  124.4 1.1 copy-done.1
  125.5 2.0 %shard_map.140 = (f32[64,2560]{1,0:T(8,128)}, f32[64,2560]{1,0:T(8,128)}) custom-call(f32[64,2560]{1,0:T(8,128)S(1)} %copy-done.1, f32[64,20,128]{2,1,0:T(8,128)S(1)} %copy-done), custom_call_target="tpu_custom_call" | custom-call | tf_op jit(solution)/shard_map/pallas_call | solution.py:606
  127.5 0.0 copy-start.2
  127.5 0.6 copy-done.2
  128.2 0.5 copy.16
Async XLA Ops:
  123.3 1.1 copy-start
  124.4 1.1 copy-start.1
  127.5 0.6 copy-start.2

commit v4 on v3

--- a/solution.py
+++ b/solution.py
@@ -104,7 +104,8 @@
     a_high, b_high = jnp.where(low, 0.0, turned), jnp.where(low, 0.0, packed)
     rows = jnp.concatenate([a_low, b_low[:32], a_high, b_high[:32], b_low[32:], b_high[32:]], 0)
     high, rest = split(rows)
-    return jnp.concatenate([high, rest], 0)
+    cut = 2 * LANES
+    return jnp.concatenate([high[:cut], rest[:cut], high[cut:], rest[cut:]], 0)
 
 
 def stiff_rows(value):
@@ -165,8 +166,9 @@
         target[:, cut] = rows_ref[cut, :].T[:M]
 
 
-def finish_kernel(block_ref, got_ref, next_ref, res_ref, rows_ref):
+def finish_kernel(block_ref, got_ref, ritz_in_ref, next_ref, res_ref, ritz_ref, rows_ref):
     next_ref[...] = block_ref[...]
+    ritz_ref[...] = ritz_in_ref[:, :M]
     unpack(got_ref, rows_ref, res_ref)
 
 
@@ -343,7 +345,7 @@
             right_ref[2 * step + core] = rows
             return 0
 
-        lax.fori_loop(0, spans // 2, body, 0, unroll=4)
+        lax.fori_loop(0, spans // 2, body, 0, unroll=8)
 
     prepare(ec)
 
@@ -365,29 +367,39 @@
 
         lax.fori_loop(0, HALF // group, body, 0, unroll=5)
 
-    transform(0)
-    transform(1)
-    transform(2)
-
-    def rotate(step, _, core):
-        j = 2 * step + core
+    def product(j, numbers, first, last):
         cut = pl.ds(pl.multiple_of(j * PAD, 8), PAD)
-        rows = jnp.concatenate([slot_ref[number, cut, :] for number in range(3)], 1)
+        rows = jnp.concatenate([slot_ref[number, cut, :] for number in numbers], 1)
         high = rows.astype(BF16).astype(F32)
         left = jnp.concatenate([high, rows - high], 0).astype(BF16)
         out = jnp.dot(
-            jnp.concatenate([left, left], 1), right_ref[j], preferred_element_type=F32
+            jnp.concatenate([left, left], 1),
+            right_ref[j, first:last],
+            preferred_element_type=F32,
         )
-        out = out[:PAD] + out[PAD:]
+        return cut, out[:PAD] + out[PAD:]
+
+    def rotate_first(step, _, core):
+        cut, out = product(2 * step + core, (0, 1), 0, 4 * LANES)
+        proj_ref[cut, :] = out
+        return 0
+
+    def rotate_last(j, _):
+        cut, out = product(j, (2,), 4 * LANES, 6 * LANES)
+        out = out + proj_ref[cut, :]
         proj_ref[cut, :] = out
         low_ref[j] = out[:REACH]
         high_ref[j] = out[HALF - REACH : HALF]
         return 0
 
-    lax.fori_loop(0, spans // 2, functools.partial(rotate, core=ec), 0, unroll=4)
+    transform(0)
+    transform(1)
+    lax.fori_loop(0, spans // 2, functools.partial(rotate_first, core=ec), 0, unroll=8)
     cross.wait_recv()
     prepare(1 - ec)
-    lax.fori_loop(0, spans // 2, functools.partial(rotate, core=1 - ec), 0, unroll=4)
+    lax.fori_loop(0, spans // 2, functools.partial(rotate_first, core=1 - ec), 0, unroll=8)
+    transform(2)
+    lax.fori_loop(0, spans, rotate_last, 0, unroll=8)
     halo = [
         send(high_ref, left_in_ref, sends.at[7], recvs.at[7], after),
         send(low_ref, right_in_ref, sends.at[8], recvs.at[8], before),
@@ -429,7 +441,6 @@
         back_block_ref.at[:, me], got_block_ref.at[me], locals_.at[9]
     )
     own_block.start()
-    give_block(1, 25)
 
     for copy in halo:
         copy.wait()
@@ -464,7 +475,7 @@
             sums_ref[pl.ds(j, 1), :] = jnp.where(side, energy, weight)
         return 0
 
-    lax.fori_loop(0, spans // 4, stiffen, 0, unroll=4)
+    lax.fori_loop(0, spans // 4, stiffen, 0, unroll=8)
 
     rest = pl.ds(0, 7)
     part_ref[0, elem] = sums_ref[pl.ds(pl.multiple_of(elem * 8, 8), 8), :]
@@ -477,13 +488,13 @@
             recvs.at[10],
             {"elem": other},
         )
-    give_block(25, 38)
+    give_block(1, 22)
     arrived(part_ref.at[0, rest], recvs.at[10])
     part_ref[1, ez] = jnp.sum(part_ref[0], 0)
     for step in range(1, 8):
         where = at(ex, lax.rem(ez + step, 8), ec)
         send(part_ref.at[1, ez], part_ref.at[1, ez], sends.at[11], recvs.at[11], where)
-    give_block(38, 51)
+    give_block(22, 43)
     arrived(part_ref.at[1, rest], recvs.at[11])
     pair = ex * 2 + ec
     part_ref[2, pair] = jnp.sum(part_ref[1], 0)
@@ -491,7 +502,7 @@
         other = lax.rem(pair + step, 8)
         where = at(other // 2, ez, lax.rem(other, 2))
         send(part_ref.at[2, pair], part_ref.at[2, pair], sends.at[12], recvs.at[12], where)
-    give_block(51, 64)
+    give_block(43, 64)
     arrived(part_ref.at[2, rest], recvs.at[12])
     total = jnp.sum(part_ref[2], 0)
     ritz = total / (pltpu.roll(total, M, 1) + 1e-06)
@@ -603,15 +614,15 @@
         jnp.asarray(left_terms(matrix.T)),
         slots,
     )
-    next_block, next_residual = pl.pallas_call(
+    next_block, next_residual, ritz = pl.pallas_call(
         finish_kernel,
-        out_shape=(shape(M, dofs), shape(M, dofs)),
-        in_specs=full(2),
-        out_specs=tuple(full(2)),
+        out_shape=(shape(M, dofs), shape(M, dofs), shape(1, M)),
+        in_specs=full(3),
+        out_specs=tuple(full(3)),
         scratch_shapes=[VMEM((dofs, LANES), F32)],
-        compiler_params=params(limit=16),
-    )(block, got)
-    return (next_block[None], next_residual[None], ritz[:, :M])
+        compiler_params=params(limit=60),
+    )(block, got, ritz)
+    return (next_block[None], next_residual[None], ritz)
 
 
 def solution(mesh):

time: 129 us -> 123 us (0.953)
  local copies, waits for them, and re-layouts: 3.35 us -> 0 us
  Pallas kernels: 125 us -> 122 us
    pallas_call x1, Pallas kernels: 123 us -> 118 us  [on_device(): pl.pallas_call(step_kernel, out_shape=(shape(M, dofs), shape(spans, HALF,...]
    unnamed x7 -> x0, local copies, waits for them, and re-layouts: 3.35 us -> none
    pallas_call x1, Pallas kernels: 2.02 us -> 3.35 us  [on_device(): pl.pallas_call(finish_kernel, out_shape=(shape(M, dofs), shape(M, dofs),...]
where the time goes in v4:
time: 123 us; the launch traced here: 122 us
  Pallas kernels  122 us (99%)
    pallas_call x1, Pallas kernels, on_device(): pl.pallas_call(step_kernel, out_shape=(shape(M, dofs), shape(spans, HALF,...  118 us
    pallas_call x1, Pallas kernels, on_device(): pl.pallas_call(finish_kernel, out_shape=(shape(M, dofs), shape(M, dofs),...  3.35 us

profile of v4, /device:TPU:1, one launch (start us, length us, event | category | flops | bytes accessed | tf_op | source)
XLA Modules:
  0.0 122.5 jit_solution(3429426161726331619)
XLA Ops:
  0.6 118.5 %shard_map.139 = (f32[64,2560]{1,0:T(8,128)}, f32[64,20,128]{2,1,0:T(8,128)}, f32[1,128]{1,0:T(1,128)}) custom-call(f32[64,2560]{1,0:T(8,128)} %bitcast.13, f32[64,2560]{1,0:T(8,128)} %bitcast.14, f32[64,2560]{1,0:T(8,128)} %bitcast.15, f32[20,128]{1,0:T(8,128)} %bitcast.17, f32[20,128]{1,0:T(8,128)} %bitcast.18, f32[20,128]{1,0:T(8,128)} %bitcast.19, ...), custom_call_target="tpu_custom_call" | custom-call | tf_op jit(solution)/shard_map/pallas_call | solution.py:568
  119.1 3.3 %shard_map.140 = (f32[64,2560]{1,0:T(8,128)}, f32[64,2560]{1,0:T(8,128)}, f32[1,64]{1,0:T(1,128)}) custom-call(f32[64,2560]{1,0:T(8,128)} %get-tuple-element.9.block_ref, f32[64,20,128]{2,1,0:T(8,128)} %get-tuple-element.10.got_ref, f32[1,128]{1,0:T(1,128)} %get-tuple-element.11.ritz_in_ref), custom_call_target="tpu_custom_call" | custom-call | tf_op jit(solution)/shard_map/pallas_call | solution.py:617

commit v5 on v4

--- a/solution.py
+++ b/solution.py
@@ -173,18 +173,22 @@
 
 
 def step_kernel(
-    x_ref,
-    w_ref,
-    p_ref,
+    x_in_ref,
+    w_in_ref,
+    p_in_ref,
     coefs_refs,
     offset_ref,
     turned_ref,
     four_ref,
     back_ref,
     slots_ref,
-    next_ref,
+    next_out_ref,
     got_res_ref,
     ritz_ref,
+    x_ref,
+    w_ref,
+    p_ref,
+    next_ref,
     pack_ref,
     got_ref,
     coef_ref,
@@ -216,7 +220,7 @@
     spans, elems = SPANS, lax.axis_size("elem")
     me, elem = lax.axis_index("span"), lax.axis_index("elem")
     ex, ez, ec = me // 16, lax.rem(me // 2, 8), lax.rem(me, 2)
-    dofs = x_ref.shape[1]
+    dofs = x_in_ref.shape[1]
     share = 2 * HALF
 
     up, down = me + 1, me + spans - 1
@@ -238,7 +242,15 @@
         signal(barrier, {"span": lax.rem(me + step, spans)})
         return 0
 
-    lax.fori_loop(1, spans, greet, 0)
+    loads = [
+        pltpu.make_async_copy(source, target, locals_.at[number])
+        for number, (source, target) in enumerate(
+            ((x_in_ref, x_ref), (w_in_ref, w_ref), (p_in_ref, p_ref)), 4
+        )
+    ]
+    for copy in loads:
+        copy.start()
+    lax.fori_loop(1, spans, greet, 0, unroll=7)
     for step in range(1, elems):
         signal(barrier, {"elem": elem_at(step)})
     signal(barrier, after)
@@ -252,6 +264,8 @@
         where = at(ex, lax.rem(ez + step, 8), ec)
         send(rot_ref, rall_ref.at[ex, ez, ec], sends.at[3], recvs.at[3], where)
 
+    for copy in loads:
+        copy.wait()
     count = dofs // LANES
     for block in range(count):
         cut = slice(block * LANES, (block + 1) * LANES)
@@ -526,6 +540,8 @@
     own_block.wait()
     arrived(got_block_ref.at[rest], recvs.at[9])
     unpack(got_block_ref, rows_ref, next_ref)
+    leave = pltpu.make_async_copy(next_ref, next_out_ref, locals_.at[7])
+    leave.start()
     own_res.wait()
     arrived(got_res_ref.at[rest], recvs.at[14])
 
@@ -539,6 +555,7 @@
         arrived(part_ref.at[stage, pl.ds(0, 7)], sends.at[10 + stage])
     arrived(all_ref.at[pl.ds(0, 7)], sends.at[13])
     arrived(got_res_ref.at[rest], sends.at[14])
+    leave.wait()
 
 
 def shape(*dims):
@@ -562,15 +579,21 @@
     matrix, links = fourier_np(spans)
 
     grid = (dofs // LANES, LANES)
-    rows = spans * PAD
+    rows = (spans + 1) * PAD
     slots = jnp.asarray(np.repeat(links[:, None], LANES, 1).astype(np.float32))
+
+    anywhere = pl.BlockSpec(memory_space=pl.ANY)
 
     block, got, ritz = pl.pallas_call(
         step_kernel,
         out_shape=(shape(M, dofs), shape(spans, HALF, LANES), shape(1, LANES)),
-        in_specs=full(3) + [full(4)] + full(5),
-        out_specs=tuple(full(3)),
+        in_specs=[anywhere] * 3 + [full(4)] + full(5),
+        out_specs=(anywhere,) + tuple(full(2)),
         scratch_shapes=[
+            VMEM((M, dofs), F32),
+            VMEM((M, dofs), F32),
+            VMEM((M, dofs), F32),
+            VMEM((M, dofs), F32),
             VMEM((2 * dofs, LANES), F32),
             VMEM((3 * HALF, spans, LANES), F32),
             VMEM((5, 24, LANES), F32),

time: 123 us -> 122 us (level)
  no operation moved by 1% of the time
where the time goes in v5:
time: 122 us
  Pallas kernels  121 us (99%)
    pallas_call x1, Pallas kernels, on_device(): pl.pallas_call(step_kernel, out_shape=(shape(M, dofs), shape(spans, HALF,...  118 us
    pallas_call x1, Pallas kernels, on_device(): pl.pallas_call(finish_kernel, out_shape=(shape(M, dofs), shape(M, dofs),...  3.35 us

profile of v5, /device:TPU:1, one launch (start us, length us, event | category | flops | bytes accessed | tf_op | source)
XLA Modules:
  0.0 122.1 jit_solution(12622172275338747787)
XLA Ops:
  0.6 118.1 %shard_map.139 = (f32[64,2560]{1,0:T(8,128)}, f32[64,20,128]{2,1,0:T(8,128)}, f32[1,128]{1,0:T(1,128)}) custom-call(f32[64,2560]{1,0:T(8,128)} %bitcast.13, f32[64,2560]{1,0:T(8,128)} %bitcast.14, f32[64,2560]{1,0:T(8,128)} %bitcast.15, f32[20,128]{1,0:T(8,128)} %bitcast.17, f32[20,128]{1,0:T(8,128)} %bitcast.18, f32[20,128]{1,0:T(8,128)} %bitcast.19, ...), custom_call_target="tpu_custom_call" | custom-call | tf_op jit(solution)/shard_map/pallas_call | solution.py:587
  118.8 3.3 %shard_map.140 = (f32[64,2560]{1,0:T(8,128)}, f32[64,2560]{1,0:T(8,128)}, f32[1,64]{1,0:T(1,128)}) custom-call(f32[64,2560]{1,0:T(8,128)} %get-tuple-element.9.block_ref, f32[64,20,128]{2,1,0:T(8,128)} %get-tuple-element.10.got_ref, f32[1,128]{1,0:T(1,128)} %get-tuple-element.11.ritz_in_ref), custom_call_target="tpu_custom_call" | custom-call | tf_op jit(solution)/shard_map/pallas_call | solution.py:640
